TPU v7x, 32 devices: a whole 2x2x4 slice. The times are simulated.
32 devices in a mesh: dp: 8 (over z, x), fsdp: 4 (over y, core).
Axes of the slice: x: 2, y: 2, z: 4, core: 2. Of those that a mesh axis runs over, the one named last changes fastest.
Arguments:
- block_in: float32 [32, 334, 1152], P(('dp', 'fsdp')), may hold values from -6 to 6
- skip_in: float32 [32, 334, 1152], P(('dp', 'fsdp')), may hold values from -6 to 6
- out_grad: float32 [32, 334, 1152], P(('dp', 'fsdp')), may hold values from -6 to 6
- caption_len: int32 [32], P(('dp', 'fsdp')), may hold values from 1 to 77
- skip_w: float32 [2654208], P(('dp', 'fsdp')), may hold values from -0.125 to 0.125
- qkv_w: float32 [3981312], P(('dp', 'fsdp')), may hold values from -0.1875 to 0.1875
- proj_w: float32 [1327104], P(('dp', 'fsdp')), may hold values from -1.5 to 1.5
- fc1_w: float32 [5308416], P(('dp', 'fsdp')), may hold values from -0.1875 to 0.1875
- fc2_w: float32 [5308416], P(('dp', 'fsdp')), may hold values from -0.09375 to 0.09375
- vectors: float32 [12672], P('dp'), may hold values from -0.9 to 1.5
Outputs:
- block_out: float32 [32, 334, 1152], P(('dp', 'fsdp'))
- in_grad: float32 [32, 334, 1152], P(('dp', 'fsdp'))
- skip_grad: float32 [32, 334, 1152], P(('dp', 'fsdp'))
- skip_w_grad: float32 [2654208], P(('dp', 'fsdp'))
- qkv_w_grad: float32 [3981312], P(('dp', 'fsdp'))
- proj_w_grad: float32 [1327104], P(('dp', 'fsdp'))
- fc1_w_grad: float32 [5308416], P(('dp', 'fsdp'))
- fc2_w_grad: float32 [5308416], P(('dp', 'fsdp'))
- vectors_grad: float32 [12672], P('dp')
All inputs are finite; a program needn't handle non-finite values.
Results may differ from a plain program's by a relative error of at most 0.012.
Values may be sent and summed in bfloat16 or wider, within the bound.
A program may use at most 320 MiB of HBM per device.

v0:
```python
import functools

import jax
import jax.numpy as jnp
from jax import lax
from jax.experimental import pallas as pl
from jax.experimental.pallas import tpu as pltpu
from jax.sharding import PartitionSpec as P

HEADS = 16
FF = 4608
CAPTION = 77


epsilon = 1e-05
masked_value = -1e30


def norm_rows(value, gain, shift):
    center = value - jnp.mean(value, -1, keepdims=True)
    spread = jnp.mean(center * center, -1, keepdims=True)
    return center * lax.rsqrt(spread + epsilon) * gain + shift


def gelu_exact(value):
    return jax.nn.gelu(value, approximate=False)


def key_valid(caption_len, length, caption):
    place = lax.broadcasted_iota(jnp.int32, (caption_len.shape[0], length), 1)
    return (place < 1 + caption_len[:, None]) | (place >= 1 + caption)


def product(left, right):
    return jnp.dot(left, right, preferred_element_type=jnp.float32)


def left_product(left, right):
    return lax.dot_general(
        left, right, (((0,), (0,)), ((), ())), preferred_element_type=jnp.float32
    )


def right_product(left, right):
    return lax.dot_general(
        left, right, (((1,), (1,)), ((), ())), preferred_element_type=jnp.float32
    )


def unpack(flat, width, hidden):
    return (
        flat[0].reshape(2 * width, width),
        flat[1].reshape(width, 3 * width),
        flat[2].reshape(width, width),
        flat[3].reshape(width, hidden),
        flat[4].reshape(hidden, width),
    )


def attention_scores(query, keys, valid, scale):
    raw = jnp.einsum("ishd,ithd->ihst", query, keys, preferred_element_type=jnp.float32) * scale
    return jnp.where(valid[:, None, None, :], raw, masked_value)


def column_sum(value):
    return jnp.sum(value.astype(jnp.float32), 0)


def flat_piece(left, right):
    grad_rows = left_product(left, right).reshape(-1)
    return grad_rows


MESH = pl.DeviceIdType.MESH
BF=jnp.bfloat16; F32=jnp.float32
SPLIT = 384


def unit_lanes(value, units, chips):
    seg = value.shape[1] // (units * chips)
    return [
        jnp.concatenate([value[:, (s * units + u) * seg : (s * units + u + 1) * seg] for s in range(chips)], 1)
        for u in range(units)
    ]


def row_loop(total, step, fn):
    def one(n, carry):
        fn(pl.ds(pl.multiple_of(n * step, step), step))
        return carry
    lax.fori_loop(0, total // step, one, 0)


def natural_lanes(units, chips):
    seg = units[0].shape[1] // chips
    return jnp.concatenate([u[:, s * seg : (s + 1) * seg] for s in range(chips) for u in units], 1)


def block_kernel(Z, wide, rows, lanes_a, length, padded,
                 cap_ref, skip_ref, qkv_ref, proj_ref, fc1_ref, fc2_ref, vec_ref, in_ref, sk_ref, og_ref,
                 out_o, in_o, sk_o, skip_g, qkv_g, proj_g, fc1_g, fc2_g, vec_o, skip_o, qp_o, fc1_o, fc2_o, j_o, h0_o,
                 skip_f, qkv_f, proj_f, fc1_f, fc2_f, own, keep, give, take, vbuf, vecs, b1s, vpart, vgot, vall, tok,
                 dtg, side, hid, am, t, m, zz, gu, gm, acc, tmp, sums, gacc, wbuf,
                 xl, xr, part, ra1, ra2, ra3, rc1, rc2, rc3,
                 send, recv, lsem, psend, precv, vsend, vrecv, isem, osem, wsem,
                 rsend, rrecv, xsend, xrecv, qsend, qrecv, ysend, yrecv, ssend, srecv, free):
    dp = lax.axis_index("dp"); f = lax.axis_index("fsdp")
    z = dp // 2; x = dp % 2; y = f // 2; c = f % 2
    o = 1 - c
    nt = wide // 128
    half = rows // 2
    chips = 4 * Z
    nz = Z - 1
    ndp = 2 * Z
    hd = wide // HEADS
    full = length // 16 * 16
    A = pl.ds(0, lanes_a); C = pl.ds(lanes_a, wide - lanes_a)
    zi = [lax.rem(z + k, Z) for k in range(1, Z)]
    zs = [(i * 2 + x, f) for i in zi]
    xp = (z * 2 + 1 - x, f)
    yp = (dp, (1 - y) * 2 + c)
    pp = (dp, y * 2 + o)
    dps = [(lax.rem(dp + k, ndp), f) for k in range(1, ndp)]
    fs = [(dp, lax.rem(f + k, 4)) for k in range(1, 4)]
    bar = pltpu.get_barrier_semaphore()
    for d in dps + fs:
        pl.semaphore_signal(bar, inc=1, device_id=d, device_id_type=MESH)
    flats = [(skip_ref, skip_f), (qkv_ref, qkv_f), (proj_ref, proj_f), (fc1_ref, fc1_f), (fc2_ref, fc2_f)]
    floads = [pltpu.make_async_copy(a, b, isem.at[n]) for n, (a, b) in enumerate(flats)]
    for cp in floads: cp.start()
    loads = [pltpu.make_async_copy(in_ref.at[:, 0, :], tok.at[0], isem.at[5]), pltpu.make_async_copy(sk_ref.at[:, 0, :], tok.at[1], isem.at[6])]
    for cp in loads: cp.start()
    def remote(src, dst, ssem, rsem, dev):
        return pltpu.make_async_remote_copy(src, dst, ssem, rsem, device_id=dev, device_id_type=MESH)
    floads[0].wait()
    for j in range(nt):
        own[0, :, 128 * j:128 * j + 128] = skip_f[pl.ds(j, rows, stride=nt), :].astype(BF)
    pl.semaphore_wait(bar, len(dps) + len(fs))

    waits = []
    def rc(i, slot, src, dst, dev):
        cp = remote(src, dst, send.at[i, slot], recv.at[i, slot], dev)
        cp.start(); waits.append(cp)
    def got(i, slot, dst):
        remote(dst, dst, send.at[i, slot], recv.at[i, slot], pp).wait_recv()
    def unit(i, cc):
        if i == 0: return skip_o.at[:, :, :, cc]
        if i in (1, 2): return qp_o.at[2 * (i - 1) + cc]
        if i in (3, 4): return fc1_o.at[2 * cc + (i - 3)]
        return fc2_o.at[2 * cc + (i - 5)]
    pc = {}
    lc = {}
    def exchange(i, first, second):
        keep[i - 1, 0:half, :] = jnp.where(c == 0, first, second)
        give[i - 1, 0:half, :] = jnp.where(c == 0, second, first)
        pc[i] = remote(give.at[i - 1], take.at[i - 1], psend.at[i - 1], precv.at[i - 1], pp)
        pc[i].start()
    def stage1(i):
        U = unit(i, c)
        if i in (1, 2, 3, 4):
            pc[i].wait_recv()
            p = keep[i - 1, 0:half, :]
            q = take[i - 1, 0:half, :]
            lo = jnp.where(c == 0, p, q); hi = jnp.where(c == 0, q, p)
            own[i, :, :] = jnp.concatenate([lo, hi], 0).astype(BF)
        lc[i] = pltpu.make_async_copy(own.at[i], U.at[z, x, y], lsem.at[i]); lc[i].start()
        rc(i, 2 * nz, own.at[i, :, C], U.at[z, x, y, :, C], yp)
        for k in range(1, Z):
            rc(i, k - 1, own.at[i, :, A], U.at[z, x, y, :, A], zs[k - 1])
    def stage2(i):
        U = unit(i, c)
        lc[i].wait()
        got(i, 2 * nz, U.at[z, x, 1 - y, :, C])
        for k in range(1, Z):
            rc(i, nz + k - 1, U.at[z, x, :, :, C], U.at[z, x, :, :, C], zs[k - 1])
        for k in range(1, Z):
            got(i, k - 1, U.at[lax.rem(z - k + Z, Z), x, y, :, A])
        L = U.at[:, x, y, :, A]
        rc(i, 2 * nz + 1, L, L, xp)
        rc(i, 2 * nz + 2, L, L, yp)
        rc(i, 2 * nz + 5, L, L, pp)
    def stage3(i):
        U = unit(i, c)
        for k in range(1, Z):
            got(i, nz + k - 1, U.at[lax.rem(z - k + Z, Z), x, :, :, C])
        L = U.at[:, x, :, :, C]
        rc(i, 2 * nz + 4, L, L, xp)
        rc(i, 2 * nz + 6, L, L, pp)
        L = U.at[:, 1 - x, y, :, A]
        got(i, 2 * nz + 1, L)
        rc(i, 2 * nz + 3, L, L, yp)
        rc(i, 2 * nz + 7, L, L, pp)
    def stage4(i):
        U = unit(i, c)
        L = U.at[:, x, 1 - y, :, A]
        got(i, 2 * nz + 2, L); rc(i, 2 * nz + 8, L, L, pp)
        L = U.at[:, 1 - x, 1 - y, :, A]
        got(i, 2 * nz + 3, L); rc(i, 2 * nz + 9, L, L, pp)
        L = U.at[:, 1 - x, :, :, C]
        got(i, 2 * nz + 4, L); rc(i, 2 * nz + 10, L, L, pp)
    def arrived(i):
        U = unit(i, 1 - c)
        got(i, 2 * nz + 5, U.at[:, x, y, :, A])
        got(i, 2 * nz + 7, U.at[:, 1 - x, y, :, A])
        got(i, 2 * nz + 8, U.at[:, x, 1 - y, :, A])
        got(i, 2 * nz + 9, U.at[:, 1 - x, 1 - y, :, A])
        got(i, 2 * nz + 6, U.at[:, x, :, :, C])
        got(i, 2 * nz + 10, U.at[:, 1 - x, :, :, C])
    def read(ref, first, stride):
        return jnp.concatenate([ref[pl.ds(first + j, half, stride=stride), :] for j in range(nt)], 1)

    stage1(0)
    vcopies = []
    vbuf[dp] = vec_ref[...]
    for k, d in enumerate(dps):
        cp = remote(vec_ref, vbuf.at[dp], vsend.at[k], vrecv.at[k], d)
        cp.start(); vcopies.append(cp)
    floads[1].wait(); floads[2].wait()
    exchange(1, read(qkv_f, 0, 3 * nt), read(qkv_f, nt, 3 * nt))
    exchange(2, read(qkv_f, 2 * nt, 3 * nt), read(proj_f, 0, nt))
    def prepare_late():
        floads[3].wait(); floads[4].wait()
        for j in range(nt):
            own[5, :, 128 * j:128 * j + 128] = fc2_f[pl.ds(j, rows, stride=nt), :].astype(BF)
            own[6, :, 128 * j:128 * j + 128] = fc2_f[pl.ds(j + nt * rows, rows, stride=nt), :].astype(BF)
        nat = jnp.concatenate([read(fc1_f, nt * v, 4 * nt) for v in range(4)], 1)
        u = unit_lanes(nat, 4, chips)
        exchange(3, u[0], u[2])
        exchange(4, u[1], u[3])

    def keep_out(n, src, dst):
        cp = pltpu.make_async_copy(src, dst, osem.at[n]); cp.start()
        return cp
    def weight(n, ref):
        pltpu.make_async_copy(ref, wbuf.at[n], wsem.at[n]).start()
    def weight_wait(k):
        pltpu.make_async_copy(wbuf.at[k], wbuf.at[k], wsem.at[k]).wait()
    def both_skip():
        for k in range(2):
            for i in range(Z // 2):
                pltpu.make_async_copy(skip_o.at[k * (Z // 2) + i], wbuf.at[k, pl.ds(2 * i, 2)], wsem.at[k]).start()
    def cols(k, l):
        return wbuf[k, :, :, :, :, l].reshape(wide, SPLIT)
    def lanes_loop(fn):
        def one(n, carry):
            fn(pl.ds(pl.multiple_of(n * SPLIT, 128), SPLIT))
            return carry
        lax.fori_loop(0, wide // SPLIT, one, 0)
    def vector(n):
        return vecs[0:1, n * wide:(n + 1) * wide]
    def put_rows(k, src):
        def one(r): tok[k, r, :] = src[r, :]
        row_loop(full, 16, one)
        if length > full: tok[k, full:length, :] = src[full:length, :]
    def norm(src, gain, shift, dst):
        def one(r):
            v = src[r, :]
            cen = v - jnp.mean(v, -1, keepdims=True)
            s = jnp.mean(cen * cen, -1, keepdims=True)
            dst[r, :] = (cen * lax.rsqrt(s + epsilon) * gain + shift).astype(BF)
        row_loop(padded, 16, one)
    def take_rows(k, dst, at):
        if padded > full: dst[at + (slice(padded - 16, padded), slice(None))] = jnp.zeros((16, wide), dst.dtype)
        def one(r): dst[at + (r, slice(None))] = tok[k, r, :].astype(dst.dtype)
        row_loop(full, 16, one)
        if length > full: dst[at + (slice(full, length), slice(None))] = tok[k, full:length, :].astype(dst.dtype)
    def inputs():
        for cp in loads: cp.wait()
        take_rows(0, dtg, (0,))
        take_rows(1, dtg, (1,))
        pltpu.make_async_copy(og_ref.at[:, 0, :], tok.at[0], isem.at[5]).start()
        def two(r):
            u = unit_lanes(jnp.concatenate([dtg[0, r, :], dtg[1, r, :]], 1), 2, chips)
            side[0, r, :] = u[0]
            side[1, r, :] = u[1]
        row_loop(padded, 16, two)
        keep_out(0, side, j_o)
    def vectors():
        for k in range(len(dps)):
            remote(vec_ref, vbuf.at[lax.rem(dp - (k + 1) + ndp, ndp)], vsend.at[k], vrecv.at[k], pp).wait_recv()
        vecs[...] = jnp.concatenate([vbuf[k] for k in range(ndp)], 1)
        b = unit_lanes(vecs[0:1, 7 * wide:11 * wide], 4, chips)
        for u in range(4): b1s[u] = b[u]
        pltpu.make_async_copy(og_ref.at[:, 0, :], tok.at[0], isem.at[5]).wait()
        take_rows(0, gm, ())
        pltpu.make_async_copy(og_ref.at[:, 0, :], tok.at[1], isem.at[6]).start()
    def first_part():
        arrived(0)
        both_skip()
        weight_wait(0); weight_wait(1)
        def one(l):
            v = jnp.dot(dtg[0], cols(0, l), preferred_element_type=F32)
            v = v + jnp.dot(dtg[1], cols(1, l), preferred_element_type=F32)
            hid[:, l] = v + vecs[0:1, pl.ds(4 * wide + l.start, SPLIT)]
        lanes_loop(one)
        norm(hid, vector(0), vector(1), am.at[0])
        keep_out(1, hid, h0_o)
    def project(n, u):
        def one(l):
            t[u, :, l] = jnp.dot(am[0], cols(n, l), preferred_element_type=F32).astype(BF)
        lanes_loop(one)
    def query_keys():
        arrived(1)
        for u in range(2): weight(u, qp_o.at[u])
        for u in range(2):
            weight_wait(u)
            project(u, u)
    def values():
        arrived(2)
        weight(0, qp_o.at[2]); weight(1, qp_o.at[3])
        weight_wait(0)
        project(0, 2)
    def window(h):
        base = pl.multiple_of(jnp.minimum((h * hd) // 128, nt - 2) * 128, 128)
        lane = lax.broadcasted_iota(jnp.int32, (1, 256), 1) + (base - h * hd)
        return pl.ds(base, 256), (lane >= 0) & (lane < hd)
    def attend(first, last):
        cap = cap_ref[0]
        key = lax.broadcasted_iota(jnp.int32, (1, padded), 1)
        live = ((key < 1 + cap) | (key >= 1 + CAPTION)) & (key < length)
        def head(h, carry):
            win, inside = window(h)
            q = jnp.where(inside, t[0, :, win].astype(F32), 0.0).astype(BF)
            s = lax.dot_general(q, t[1, :, win], (((1,), (1,)), ((), ())), preferred_element_type=F32) * hd ** (-0.5)
            s = jnp.where(live, s, masked_value)
            e = jnp.exp(s - jnp.max(s, -1, keepdims=True))
            p = (e / jnp.sum(e, -1, keepdims=True)).astype(BF)
            v = jnp.dot(p, t[2, :, win], preferred_element_type=F32)
            am[1, :, win] = jnp.where(inside, v, am[1, :, win].astype(F32)).astype(BF)
            return carry
        lax.fori_loop(first, last, head, 0)
    def second_part():
        weight_wait(1)
        pltpu.make_async_copy(hid, h0_o, osem.at[1]).wait()
        def one(l):
            v = jnp.dot(am[1], cols(1, l), preferred_element_type=F32)
            h = hid[:, l] + (v + vecs[0:1, pl.ds(5 * wide + l.start, SPLIT)])
            hid[:, l] = h
            acc[:, l] = h + vecs[0:1, pl.ds(6 * wide + l.start, SPLIT)]
        lanes_loop(one)
        norm(hid, vector(2), vector(3), m)
    def widen_load(i):
        arrived(i)
        for k in range(2): weight(k, fc1_o.at[2 * k + i - 3])
    def widen(k, u):
        weight_wait(k)
        def one(l):
            tmp[:, l] = jnp.dot(m[...], cols(k, l), preferred_element_type=F32)
        lanes_loop(one)
        def two(r):
            v = tmp[r, :] + b1s[u]
            cdf = 0.5 * (1.0 + lax.erf(v * 0.7071067811865476))
            pdf = jnp.exp(-0.5 * v * v) * 0.3989422804014327
            zz[u, r, :] = (v * cdf).astype(BF)
            gu[u, r, :] = (cdf + v * pdf).astype(BF)
        row_loop(padded, 16, two)
    def narrow_load(i):
        arrived(i)
        for k in range(2): weight(k, fc2_o.at[2 * k + i - 5])
    def narrow(k, u):
        weight_wait(k)
        tmp[...] = jnp.zeros_like(tmp)
        def one(l):
            w = cols(k, l)
            acc[:, l] += jnp.dot(zz[u], w, preferred_element_type=F32)
            tmp[...] += lax.dot_general(gm[:, l], w, (((1,), (1,)), ((), ())), preferred_element_type=F32)
        lanes_loop(one)
        def two(r):
            gu[u, r, :] = (tmp[r, :] * gu[u, r, :].astype(F32)).astype(BF)
        row_loop(padded, 16, two)

    xcopies = {}
    def swap(n, src, dst):
        xcopies[n] = remote(src, dst, xsend.at[n], xrecv.at[n], pp)
        xcopies[n].start()
    nb = 4
    started = {j: [] for j in range(7)}
    def sc(j, slot, src, dst, dev):
        cp = remote(src, dst, rsend.at[j, slot], rrecv.at[j, slot], dev)
        cp.start(); started[j].append(cp)
    def came(j, slot, dst):
        remote(dst, dst, rsend.at[j, slot], rrecv.at[j, slot], pp).wait_recv()
    need = [(0, 1), (2,), (3, 4), (5,), (6, 7), (8, 9), (10, 11)]
    def operands(j):
        if j < 2: return zz.at[2 * c + j], gm, xl.at[j], xr.at[0]
        if j < 4: return m, gu.at[2 * c + j - 2], xl.at[2], xr.at[j - 1]
        if j == 4: return am.at[c], dtg.at[2 + c], xl.at[0], xr.at[0]
        if j == 5: return am.at[0], dtg.at[c], xl.at[1], xr.at[1]
        return side.at[0], side.at[1], xl.at[2], xr.at[2]
    def reduce1(j):
        for n in need[j]: xcopies[n].wait_recv()
        if j >= nb:
            for cp in started[j - nb]: cp.wait_send()
        b = j % nb
        D = part.at[b]
        l1, r1, l2, r2 = operands(j)
        step = wide - lanes_a
        dims = (((0,), (0,)), ((), ()))
        def chunk(n, carry):
            lanes = pl.ds(pl.multiple_of(n * step, 128), step)
            r = lax.dot_general(l1[...], r1[:, lanes], dims, preferred_element_type=F32)
            r = r + lax.dot_general(l2[...], r2[:, lanes], dims, preferred_element_type=F32)
            D[:, :, :, :, lanes] = r.reshape(Z, 2, 2, rows, step).astype(BF)
            return carry
        lax.fori_loop(0, wide // step, chunk, 0)
        sc(j, 0, D.at[:, 1 - x, 1 - y, :, A], ra1.at[b, 0], yp)
        sc(j, 2, D.at[:, 1 - x, :, :, C], rc1.at[b], xp)
        sc(j, 1, D.at[:, x, 1 - y, :, A], ra1.at[b, 1], yp)
    def reduce2(j):
        b = j % nb
        D = part.at[b]
        came(j, 0, ra1.at[b, 0])
        for zz in range(Z):
            va = D.at[zz, 1 - x, y, :, A]
            va[...] = (va[...].astype(F32) + ra1[b, 0, zz].astype(F32)).astype(BF)
        sc(j, 3, D.at[:, 1 - x, y, :, A], ra2.at[b], xp)
        came(j, 2, rc1.at[b])
        for zz in range(Z):
            for yy in range(2):
                va = D.at[zz, x, yy, :, C]
                va[...] = (va[...].astype(F32) + rc1[b, zz, yy].astype(F32)).astype(BF)
        for k in range(nz):
            sc(j, 4 + k, D.at[zi[k], x, :, :, C], rc2.at[b, k], zs[k])
    def reduce3(j):
        b = j % nb
        D = part.at[b]
        came(j, 1, ra1.at[b, 1])
        came(j, 3, ra2.at[b])
        for zz in range(Z):
            va = D.at[zz, x, y, :, A]
            va[...] = (va[...].astype(F32) + ra1[b, 1, zz].astype(F32) + ra2[b, zz].astype(F32)).astype(BF)
        for k in range(nz):
            sc(j, 4 + nz + k, D.at[zi[k], x, y, :, A], ra3.at[b, k], zs[k])
        for k in range(nz):
            came(j, 4 + k, rc2.at[b, k])
        for yy in range(2):
            va = D.at[z, x, yy, :, C]
            s = va[...].astype(F32)
            for k in range(nz):
                s = s + rc2[b, k, yy].astype(F32)
            va[...] = s.astype(BF)
        sc(j, 4 + 2 * nz, D.at[z, x, 1 - y, :, C], rc3.at[b], yp)
    pcopies = {}
    def lay(ref, val, first, stride, n):
        for i in range(val.shape[1] // 128):
            ref[pl.ds(first + i, n, stride=stride), :] = val[:, 128 * i:128 * i + 128]
    def reduce4(j):
        b = j % nb
        D = part.at[b]
        for k in range(nz):
            came(j, 4 + nz + k, ra3.at[b, k])
        came(j, 4 + 2 * nz, rc3.at[b])
        p = D[z, x, y, :, 0:lanes_a].astype(F32)
        for k in range(nz):
            p = p + ra3[b, k].astype(F32)
        q = D[z, x, y, :, lanes_a:wide].astype(F32) + rc3[b].astype(F32)
        v = jnp.concatenate([p, q], 1)
        if j in (0, 1):
            lay(fc2_f, v, j * rows * nt, nt, rows)
            if j == 1: keep_out(9, fc2_f, fc2_g)
        elif j == 6:
            lay(skip_f, v, 0, nt, rows)
            keep_out(5, skip_f, skip_g)
        else:
            lo = v[0:half]; hi = v[half:rows]
            keep[j - 2, 0:half, :] = jnp.where(c == 0, lo, hi)
            give[j - 2, 0:half, :] = jnp.where(c == 0, hi, lo)
            cp = remote(give.at[j - 2], take.at[j - 2], qsend.at[j - 2], qrecv.at[j - 2], pp)
            cp.start(); pcopies[j] = cp
    def both(j):
        pcopies[j].wait_recv()
        p = keep[j - 2, 0:half, :]; q = take[j - 2, 0:half, :]
        return jnp.where(c == 0, p, q), jnp.where(c == 0, q, p)
    def reduce5(j):
        if j == 3:
            p, q = both(2), both(3)
            lay(fc1_f, natural_lanes([p[0], q[0], p[1], q[1]], chips), 0, 4 * nt, half)
            keep_out(8, fc1_f, fc1_g)
        elif j == 5:
            first, second = both(5)
            lay(qkv_f, first, 0, 3 * nt, half)
            lay(qkv_f, second, nt, 3 * nt, half)
            keep_out(6, qkv_f, qkv_g)
        elif j == 4:
            first, second = both(4)
            lay(qkv_f, first, 2 * nt, 3 * nt, half)
            lay(proj_f, second, 0, nt, half)
            keep_out(7, proj_f, proj_g)


    def zero(n): gacc[n] = jnp.zeros((8, wide), F32)
    def add_rows(n, v):
        gacc[n] += v[0:8] + v[8:16]
    def close(n):
        return jnp.sum(gacc[n], 0, keepdims=True)
    def column_sums(src):
        zero(0)
        def one(r): add_rows(0, src[r, :].astype(F32))
        row_loop(padded, 16, one)
        return close(0)
    def norm_back(dy, src, gain, fn):
        zero(0); zero(1); zero(2)
        def one(r):
            d = dy[r, :]
            v = src[r, :]
            cen = v - jnp.mean(v, -1, keepdims=True)
            rs = lax.rsqrt(jnp.mean(cen * cen, -1, keepdims=True) + epsilon)
            xh = cen * rs
            dx = d * gain
            g = rs * (dx - jnp.mean(dx, -1, keepdims=True) - xh * jnp.mean(dx * xh, -1, keepdims=True))
            add_rows(0, d * xh)
            add_rows(1, d)
            fn(r, g)
        row_loop(padded, 16, one)
    def turned(lhs, n, fresh):
        if fresh: tmp[...] = jnp.zeros_like(tmp)
        def one(l):
            tmp[...] += lax.dot_general(lhs[:, l], cols(n, l), (((1,), (1,)), ((), ())), preferred_element_type=F32)
        lanes_loop(one)
    def widen_back(us):
        for i, u in enumerate(us):
            weight_wait(i)
            turned(gu.at[u], i, u == 0)
            sums[7 + u] = column_sums(gu.at[u])
    def widen_back_load(us):
        for i, u in enumerate(us): weight(i, fc1_o.at[u])
    def norm_two():
        weight(0, qp_o.at[3])
        pltpu.make_async_copy(og_ref.at[:, 0, :], tok.at[1], isem.at[6]).wait()
        take_rows(1, acc, ())
        def fn(r, g):
            s = acc[r, :] + g
            acc[r, :] = s
            b = s.astype(BF)
            dtg[3, r, :] = b
            add_rows(2, b.astype(F32))
        norm_back(tmp, hid, vector(2), fn)
        sums[2] = close(0); sums[3] = close(1); sums[5] = close(2)
        pltpu.make_async_copy(h0_o, hid, isem.at[5]).start()
        sums[6] = column_sums(gm)
        weight_wait(0)
        turned(dtg.at[3], 0, True)
        def two(r): side[0, r, :] = tmp[r, :].astype(BF)
        row_loop(padded, 16, two)
    def attend_back(first, last):
        cap = cap_ref[0]
        key = lax.broadcasted_iota(jnp.int32, (padded, 1), 0)
        live = ((key < 1 + cap) | (key >= 1 + CAPTION)) & (key < length)
        def head(h, carry):
            win, inside = window(h)
            q = jnp.where(inside, t[0, :, win].astype(F32), 0.0).astype(BF)
            k = t[1, :, win]
            g = jnp.where(inside, side[0, :, win].astype(F32), 0.0).astype(BF)
            s = lax.dot_general(k, q, (((1,), (1,)), ((), ())), preferred_element_type=F32) * hd ** (-0.5)
            s = jnp.where(live, s, masked_value)
            e = jnp.exp(s - jnp.max(s, 0, keepdims=True))
            p = e * (1.0 / jnp.sum(e, 0, keepdims=True))
            d = lax.dot_general(t[2, :, win], g, (((1,), (1,)), ((), ())), preferred_element_type=F32)
            ds = (p * (d - jnp.sum(p * d, 0, keepdims=True))).astype(BF)
            dq = lax.dot_general(ds, k, (((0,), (0,)), ((), ())), preferred_element_type=F32) * hd ** (-0.5)
            dk = jnp.dot(ds, q, preferred_element_type=F32) * hd ** (-0.5)
            dv = jnp.dot(p.astype(BF), g, preferred_element_type=F32)
            for i, v in enumerate((dq, dk, dv)):
                dtg[i, :, win] = jnp.where(inside, v, dtg[i, :, win].astype(F32)).astype(BF)
            return carry
        lax.fori_loop(first, last, head, 0)
    def late_left():
        pl.semaphore_signal(free, inc=1, device_id=pp, device_id_type=MESH)
        pl.semaphore_wait(free, 1)
        pltpu.make_async_copy(side, j_o, osem.at[0]).wait()
        swap(6, am.at[o], xl.at[0])
        swap(8, am.at[0], xl.at[1])
        swap(10, j_o.at[o], xl.at[2])
    def late_right():
        swap(7, dtg.at[2 + o], xr.at[0])
        swap(9, dtg.at[o], xr.at[1])
        pltpu.make_async_copy(j_o.at[c], side.at[0], isem.at[7]).start()
        weight(0, qp_o.at[0]); weight(1, qp_o.at[1])
    def project_back():
        for i in range(3):
            weight_wait(i % 2)
            turned(dtg.at[i], i % 2, i == 0)
            if i == 0: weight(0, qp_o.at[2])
    def norm_one():
        pltpu.make_async_copy(h0_o, hid, isem.at[5]).wait()
        both_skip()
        def fn(r, g):
            b = (acc[r, :] + g).astype(BF)
            side[1, r, :] = b
            add_rows(2, b.astype(F32))
        norm_back(tmp, hid, vector(0), fn)
        sums[0] = close(0); sums[1] = close(1); sums[4] = close(2)
        swap(11, side.at[1], xr.at[2])
    def join_back(i, dst):
        weight_wait(i)
        turned(side.at[1], i, True)
        put_rows(i, tmp)
        keep_out(3 + i, tok.at[i], dst.at[:, 0, :])
    nv = vpart.shape[2]
    def vec_send():
        total = jnp.concatenate([sums[i] for i in range(7)] + [natural_lanes([sums[7 + u] for u in range(4)], chips)], 1)
        for k in range(ndp): vpart[k] = total[:, k * nv:(k + 1) * nv]
        for k, d in enumerate(dps):
            cp = remote(vpart.at[d[0]], vgot.at[k], ysend.at[k], yrecv.at[k], d)
            cp.start(); vcopies.append(cp)
    def vec_first():
        s = vpart[dp]
        for k in range(len(dps)):
            remote(vgot.at[k], vgot.at[k], ysend.at[k], yrecv.at[k], pp).wait_recv()
            s = s + vgot[k]
        vall[f] = s
        for k, d in enumerate(fs):
            cp = remote(vall.at[f], vall.at[f], ssend.at[k], srecv.at[k], d)
            cp.start(); vcopies.append(cp)
    def vec_last():
        for k in range(3):
            src = lax.rem(f - (k + 1) + 4, 4)
            remote(vall.at[src], vall.at[src], ssend.at[k], srecv.at[k], pp).wait_recv()
        vec_o[...] = vall[0] + vall[1] + vall[2] + vall[3]

    stage2(0)
    prepare_late()
    stage1(1)
    stage3(0)
    inputs()
    vectors()
    stage2(1); stage1(2)
    stage3(1); stage4(0)
    first_part()
    stage2(2); stage1(3)
    stage3(2); stage4(1)
    query_keys()
    stage2(3); stage1(4)
    stage3(3); stage4(2)
    values()
    attend(0, 4)
    stage2(4); stage1(5)
    attend(4, 11)
    stage3(4); stage4(3)
    attend(11, 16)
    second_part()
    stage2(5); stage1(6)
    widen_load(3)
    widen(0, 0)
    stage3(5); stage4(4)
    widen(1, 2)
    stage2(6)
    widen_load(4)
    widen(0, 1)
    stage3(6); stage4(5)
    widen(1, 3)
    for cp in pc.values(): cp.wait_send()
    swap(0, zz.at[2 * o], xl.at[0])
    swap(1, gm, xr.at[0])
    swap(2, zz.at[2 * o + 1], xl.at[1])
    swap(3, m, xl.at[2])
    narrow_load(5)
    reduce1(0)
    narrow(0, 0)
    stage4(6)
    narrow(1, 2)
    swap(4, gu.at[2 * o], xr.at[1])
    reduce1(1); reduce2(0)
    narrow_load(6)
    narrow(0, 1)
    narrow(1, 3)
    swap(5, gu.at[2 * o + 1], xr.at[2])
    widen_back_load((0, 1))
    reduce1(2); reduce2(1); reduce3(0)
    put_rows(0, acc)
    keep_out(2, tok.at[0], out_o.at[:, 0, :])
    widen_back((0, 1))
    widen_back_load((2, 3))
    reduce1(3)
    widen_back((2, 3))
    reduce2(2); reduce3(1); reduce4(0)
    late_left()
    norm_two()
    attend_back(0, 4)
    reduce2(3); reduce3(2); reduce4(1)
    attend_back(4, 10)
    reduce3(3); reduce4(2)
    attend_back(10, 16)
    late_right()
    reduce1(4); reduce4(3)
    reduce1(5); reduce2(4)
    project_back()
    norm_one()
    vec_send()
    reduce2(5); reduce3(4)
    pltpu.make_async_copy(j_o.at[c], side.at[0], isem.at[7]).wait()
    reduce1(6)
    vec_first()
    pltpu.make_async_copy(tok.at[0], out_o.at[:, 0, :], osem.at[2]).wait()
    join_back(0, in_o)
    reduce3(5); reduce4(4)
    join_back(1, sk_o)
    reduce5(3)
    reduce2(6)
    vec_last()
    reduce4(5); reduce5(4)
    reduce3(6)
    reduce5(5)
    reduce4(6)
    for k in (0, 1): pltpu.make_async_copy(tok.at[k], (in_o, sk_o)[k].at[:, 0, :], osem.at[3 + k]).wait()
    for n, (a, b) in zip((5, 6, 7, 8, 9), ((skip_f, skip_g), (qkv_f, qkv_g), (proj_f, proj_g), (fc1_f, fc1_g), (fc2_f, fc2_g))):
        pltpu.make_async_copy(a, b, osem.at[n]).wait()
    for j in range(3, 7):
        for cp in started[j]: cp.wait_send()
    for cp in waits: cp.wait_send()
    for cp in pcopies.values(): cp.wait_send()
    for cp in vcopies: cp.wait_send()
    for cp in xcopies.values(): cp.wait_send()


def block(cap, skip, qkv, proj, fc1, fc2, vectors, block_in, skip_in, out_grad, dpn):
    _, length, wide = block_in.shape
    Z = dpn // 2; rows = skip.shape[0] // wide
    padded = -(-length // 16) * 16
    lanes_a = (wide // 128 * 2 + 1) // 3 * 128
    lc = wide - lanes_a
    U = (Z, 2, 2, rows, wide)
    hbm = pl.BlockSpec(memory_space=pl.ANY); vm = pl.BlockSpec(memory_space=pltpu.VMEM)
    ns = 2 * (Z - 1) + 11
    nr = 2 * (Z - 1) + 5
    nv = vectors.shape[0]
    D = pltpu.SemaphoreType.DMA
    V = pltpu.VMEM
    hp = -(-rows // 2 // 8) * 8
    S = jax.ShapeDtypeStruct
    act = (padded, wide)
    flat = [(w.shape[0] // 128, 128) for w in (skip, qkv, proj, fc1, fc2)]
    tokens = (length, 1, wide)
    nb = 4
    nz = Z - 1
    res = pl.pallas_call(
        functools.partial(block_kernel, Z, wide, rows, lanes_a, length, padded),
        out_shape=(S(tokens, F32),) * 3 + tuple(S(s, F32) for s in flat) + (S((1, nv), F32),
                   S((Z, 2, 2, 2, rows, wide), BF), S((4,) + U, BF), S((4,) + U, BF), S((4,) + U, BF), S((2,) + act, BF), S(act, F32)),
        in_specs=[pl.BlockSpec(memory_space=pltpu.SMEM)] + [hbm] * 5 + [vm] + [hbm] * 3,
        out_specs=(hbm,) * 8 + (vm,) + (hbm,) * 6,
        scratch_shapes=[V(s, F32) for s in flat] + [
                        V((7, rows, wide), BF), V((4, hp, wide), F32), V((4, hp, wide), F32), V((4, hp, wide), F32),
                        V((dpn, 1, nv), F32), V((1, nv * dpn), F32), V((4, 1, wide), F32), V((dpn, 1, nv), F32), V((dpn - 1, 1, nv), F32), V((4, 1, nv), F32),
                        V((2, length, wide), F32),
                        V((4,) + act, BF), V((2,) + act, BF), V(act, F32), V((2,) + act, BF), V((3,) + act, BF), V(act, BF), V((4,) + act, BF), V((4,) + act, BF), V(act, BF),
                        V(act, F32), V(act, F32), V((11, 1, wide), F32), V((3, 8, wide), F32), V((2,) + U, BF),
                        V((3,) + act, BF), V((3,) + act, BF), V((nb,) + U, BF),
                        V((nb, 2, Z, rows, lanes_a), BF), V((nb, Z, rows, lanes_a), BF), V((nb, nz, rows, lanes_a), BF),
                        V((nb, Z, 2, rows, lc), BF), V((nb, nz, 2, rows, lc), BF), V((nb, rows, lc), BF),
                        D((7, ns)), D((7, ns)), D((7,)), D((4,)), D((4,)), D((dpn - 1,)), D((dpn - 1,)), D((8,)), D((10,)), D((2,)),
                        D((7, nr)), D((7, nr)), D((12,)), D((12,)), D((4,)), D((4,)), D((dpn - 1,)), D((dpn - 1,)), D((3,)), D((3,)), pltpu.SemaphoreType.REGULAR],
        compiler_params=pltpu.CompilerParams(collective_id=0, has_side_effects=True, vmem_limit_bytes=67043328),
        name="block",
    )(cap, *(w.reshape(-1, 128) for w in (skip, qkv, proj, fc1, fc2)), vectors.reshape(1, nv),
      *(v.reshape(tokens) for v in (block_in, skip_in, out_grad)))
    shape = block_in.shape
    return tuple(r.reshape(shape) for r in res[:3]) + tuple(r.reshape(-1) for r in res[3:9])


def whole_rows(width, dp, fsdp, items, heads, hidden):
    return (
        fsdp == 4 and dp % 2 == 0 and width % (dp * 16) == 0 and items == 1 and hidden == 4 * width
        and width % SPLIT == 0 and width // heads <= 128
    )


def body(block_in, skip_in, out_grad, caption_len, skip_w, qkv_w, proj_w, fc1_w, fc2_w, vectors):
    items, length, width = block_in.shape
    if whole_rows(width, lax.axis_size("dp"), lax.axis_size("fsdp"), items, HEADS, FF):
        return block(
            caption_len, skip_w, qkv_w, proj_w, fc1_w, fc2_w, vectors, block_in, skip_in, out_grad,
            lax.axis_size("dp"),
        )
    heads = HEADS
    head_dim = width // heads
    hidden = FF
    rows = items * length
    scale = head_dim ** (-0.5)
    gathered = (
        lax.all_gather(skip_w.astype(jnp.bfloat16), ("dp", "fsdp"), axis=0, tiled=True),
        lax.all_gather(qkv_w.astype(jnp.bfloat16), ("dp", "fsdp"), axis=0, tiled=True),
        lax.all_gather(proj_w.astype(jnp.bfloat16), ("dp", "fsdp"), axis=0, tiled=True),
        lax.all_gather(fc1_w.astype(jnp.bfloat16), ("dp", "fsdp"), axis=0, tiled=True),
        lax.all_gather(fc2_w.astype(jnp.bfloat16), ("dp", "fsdp"), axis=0, tiled=True),
    )
    skip_m, qkv_m, proj_m, fc1_m, fc2_m = unpack(gathered, width, hidden)
    vec = lax.all_gather(vectors, "dp", axis=0, tiled=True)
    gain_one = vec[0:width]
    shift_one = vec[width : 2 * width]
    gain_two = vec[2 * width : 3 * width]
    shift_two = vec[3 * width : 4 * width]
    skip_bias = vec[4 * width : 5 * width]
    proj_bias = vec[5 * width : 6 * width]
    fc2_bias = vec[6 * width : 7 * width]
    fc1_bias = vec[7 * width :]
    valid = key_valid(caption_len, length, CAPTION)
    joined = jnp.concatenate([block_in, skip_in], -1).reshape(rows, 2 * width).astype(jnp.bfloat16)
    first = product(joined, skip_m) + skip_bias
    normed_one = norm_rows(first, gain_one, shift_one).astype(jnp.bfloat16)
    triple = (
        product(normed_one, qkv_m).astype(jnp.bfloat16).reshape(items, length, 3, heads, head_dim)
    )
    query = triple[:, :, 0]
    keys = triple[:, :, 1]
    values = triple[:, :, 2]
    scores = attention_scores(query, keys, valid, scale)
    top = jnp.max(scores, -1, keepdims=True)
    expd = jnp.exp(scores - top)
    total = jnp.sum(expd, -1, keepdims=True)
    probs = expd / total
    log_total = top + jnp.log(total)
    mixed = (
        jnp.einsum(
            "ihst,ithd->ishd",
            probs.astype(jnp.bfloat16),
            values,
            preferred_element_type=jnp.float32,
        )
        .astype(jnp.bfloat16)
        .reshape(rows, width)
    )
    second = first + (product(mixed, proj_m) + proj_bias)
    normed_two = norm_rows(second, gain_two, shift_two).astype(jnp.bfloat16)
    inner = product(normed_two, fc1_m) + fc1_bias
    active = gelu_exact(inner).astype(jnp.bfloat16)
    block_out = second + (product(active, fc2_m) + fc2_bias)
    again = (
        lax.all_gather(skip_w.astype(jnp.bfloat16), ("dp", "fsdp"), axis=0, tiled=True),
        lax.all_gather(qkv_w.astype(jnp.bfloat16), ("dp", "fsdp"), axis=0, tiled=True),
        lax.all_gather(proj_w.astype(jnp.bfloat16), ("dp", "fsdp"), axis=0, tiled=True),
        lax.all_gather(fc1_w.astype(jnp.bfloat16), ("dp", "fsdp"), axis=0, tiled=True),
        lax.all_gather(fc2_w.astype(jnp.bfloat16), ("dp", "fsdp"), axis=0, tiled=True),
    )
    skip_m, qkv_m, proj_m, fc1_m, fc2_m = unpack(again, width, hidden)
    grad_out = out_grad.reshape(rows, width)
    grad_mlp = grad_out.astype(jnp.bfloat16)
    d_fc2_bias = column_sum(grad_mlp)
    d_active = right_product(grad_mlp, fc2_m)
    gelu_value, gelu_pull = jax.vjp(gelu_exact, inner)
    grad_inner = gelu_pull(d_active)[0].astype(jnp.bfloat16)
    d_fc1_bias = column_sum(grad_inner)
    d_normed_two = right_product(grad_inner, fc1_m)
    norm_value_two, norm_pull_two = jax.vjp(norm_rows, second, gain_two, shift_two)
    d_second_norm, d_gain_two, d_shift_two = norm_pull_two(d_normed_two)
    grad_second = grad_out + d_second_norm
    grad_attn = grad_second.astype(jnp.bfloat16)
    d_proj_bias = column_sum(grad_attn)
    grad_mixed = (
        right_product(grad_attn, proj_m)
        .astype(jnp.bfloat16)
        .reshape(items, length, heads, head_dim)
    )
    again_scores = attention_scores(query, keys, valid, scale)
    again_probs = jnp.exp(again_scores - log_total)
    d_probs = jnp.einsum("ishd,ithd->ihst", grad_mixed, values, preferred_element_type=jnp.float32)
    inner_sum = jnp.sum(again_probs * d_probs, -1, keepdims=True)
    grad_scores = (again_probs * (d_probs - inner_sum)).astype(jnp.bfloat16)
    d_query = (
        jnp.einsum("ihst,ithd->ishd", grad_scores, keys, preferred_element_type=jnp.float32) * scale
    )
    d_keys = (
        jnp.einsum("ihst,ishd->ithd", grad_scores, query, preferred_element_type=jnp.float32)
        * scale
    )
    d_values = jnp.einsum(
        "ihst,ishd->ithd",
        again_probs.astype(jnp.bfloat16),
        grad_mixed,
        preferred_element_type=jnp.float32,
    )
    grad_triple = (
        jnp.stack([d_query, d_keys, d_values], 2).astype(jnp.bfloat16).reshape(rows, 3 * width)
    )
    d_normed_one = right_product(grad_triple, qkv_m)
    norm_value_one, norm_pull_one = jax.vjp(norm_rows, first, gain_one, shift_one)
    d_first_norm, d_gain_one, d_shift_one = norm_pull_one(d_normed_one)
    grad_first = (grad_second + d_first_norm).astype(jnp.bfloat16)
    d_skip_bias = column_sum(grad_first)
    grad_joined = right_product(grad_first, skip_m).reshape(items, length, 2 * width)
    in_grad = grad_joined[:, :, 0:width]
    skip_grad = grad_joined[:, :, width:]
    owners = lax.axis_size(("dp", "fsdp"))
    pairs = (
        (joined, grad_first),
        (normed_one, grad_triple),
        (mixed, grad_attn),
        (normed_two, grad_inner),
        (active, grad_mlp),
    )
    shard_sizes = [pair[0].shape[1] * pair[1].shape[1] // owners for pair in pairs]
    blocks = []
    for pair, owner_share in zip(pairs, shard_sizes):
        blocks.append(
            flat_piece(pair[0], pair[1]).reshape(1 * lax.axis_size(("dp", "fsdp")), owner_share)
        )
    owned = lax.psum_scatter(
        jnp.concatenate(blocks, 1), ("dp", "fsdp"), scatter_dimension=0, tiled=True
    ).reshape(-1)
    pieces = []
    offset = 0
    for share in shard_sizes:
        pieces.append(owned[offset : offset + share])
        offset = offset + share
    vec_grad = jnp.concatenate(
        [
            d_gain_one,
            d_shift_one,
            d_gain_two,
            d_shift_two,
            d_skip_bias,
            d_proj_bias,
            d_fc2_bias,
            d_fc1_bias,
        ]
    )
    vec_rows = lax.psum_scatter(vec_grad, "dp", scatter_dimension=0, tiled=True)
    vec_total = lax.psum(vec_rows, "fsdp")
    return (
        block_out.reshape(items, length, width),
        in_grad,
        skip_grad,
        pieces[0],
        pieces[1],
        pieces[2],
        pieces[3],
        pieces[4],
        vec_total,
    )


def solution(mesh):
    placed = (
        P(("dp", "fsdp"), None, None),
        P(("dp", "fsdp"), None, None),
        P(("dp", "fsdp"), None, None),
        P(("dp", "fsdp")),
        P(("dp", "fsdp")),
        P(("dp", "fsdp")),
        P(("dp", "fsdp")),
        P(("dp", "fsdp")),
        P(("dp", "fsdp")),
        P("dp"),
    )
    return jax.shard_map(
        body,
        mesh=mesh,
        in_specs=placed,
        out_specs=(
            P(("dp", "fsdp"), None, None),
            P(("dp", "fsdp"), None, None),
            P(("dp", "fsdp"), None, None),
            P(("dp", "fsdp")),
            P(("dp", "fsdp")),
            P(("dp", "fsdp")),
            P(("dp", "fsdp")),
            P(("dp", "fsdp")),
            P("dp"),
        ),
        check_vma=False,
    )
```

profile of v0, /device:TPU:0, one launch (start us, length us, event | category | flops | bytes accessed | tf_op | source)
XLA Modules:
  0.0 388.1 jit_solution(11258054951771697657)
XLA Ops:
  1.3 1.3 reshape.77.vec_ref
  2.6 373.3 %block.1 = (f32[334,1,1152]{2,1,0:T(1,128)}, f32[334,1,1152]{2,1,0:T(1,128)}, f32[334,1,1152]{2,1,0:T(1,128)}, f32[648,128]{1,0:T(8,128)}, f32[972,128]{1,0:T(8,...) custom-call(s32[1]{0:T(128)S(6)} %copy.27.cap_ref, ...), custom_call_target="tpu_custom_call" | custom-call | tf_op jit(solution)/shard_map/block/pallas_call | solution.py:736
  375.9 1.3 reduce
  377.2 0.0 copy-start.1
  377.2 3.7 copy.28
  380.9 0.0 copy-done.1
  380.9 0.0 copy-start
  380.9 1.1 copy.29
  382.0 0.8 copy-done
  382.9 0.0 copy-start.5
  382.9 0.0 copy-start.4
  382.9 1.1 copy.30
  384.0 0.0 copy-done.5
  384.0 0.0 copy-start.6
  384.0 0.0 copy-start.3
  384.0 0.0 copy-start.2
  384.0 0.7 copy.31
  384.8 0.0 copy-done.4
  384.8 0.8 copy.32
  385.6 0.0 copy-done.6
  385.6 0.7 copy.33
  386.3 0.0 copy-done.3
  386.3 0.9 copy.34
  387.2 0.0 copy-done.2
  387.2 0.9 copy.35
Async XLA Ops:
  377.2 3.7 copy-start.1
  380.9 2.0 copy-start
  382.9 1.2 copy-start.5
  382.9 1.9 copy-start.4
  384.0 1.6 copy-start.6
  384.0 2.3 copy-start.3
  384.0 3.1 copy-start.2
where the time goes:
time: 390 us; the launch traced here: 388 us
  Pallas kernels  373 us (96%)
  local copies, waits for them, and re-layouts  12.1 us (3%)
    pallas_call x1, Pallas kernels, block(): pl.pallas_call(functools.partial(block_kernel, Z, wide, rows, lanes_a, le...  373 us
    unnamed x22, local copies, waits for them, and re-layouts  10.8 us

commit v1 on v0

--- a/solution.py
+++ b/solution.py
@@ -1,4 +1,5 @@
 import functools
+import math
 
 import jax
 import jax.numpy as jnp
@@ -96,12 +97,12 @@
     return jnp.concatenate([u[:, s * seg : (s + 1) * seg] for s in range(chips) for u in units], 1)
 
 
-def block_kernel(Z, wide, rows, lanes_a, length, padded,
+def block_kernel(Z, wide, rows, tiles, length, padded,
                  cap_ref, skip_ref, qkv_ref, proj_ref, fc1_ref, fc2_ref, vec_ref, in_ref, sk_ref, og_ref,
                  out_o, in_o, sk_o, skip_g, qkv_g, proj_g, fc1_g, fc2_g, vec_o, skip_o, qp_o, fc1_o, fc2_o, j_o, h0_o,
                  skip_f, qkv_f, proj_f, fc1_f, fc2_f, own, keep, give, take, vbuf, vecs, b1s, vpart, vgot, vall, tok,
                  dtg, side, hid, am, t, m, zz, gu, gm, acc, tmp, sums, gacc, wbuf,
-                 xl, xr, part, ra1, ra2, ra3, rc1, rc2, rc3,
+                 xl, xr, part, ra1, ra2, ra3, raf, rc1, rc2, rcf, rc3, rb1, rbf, rb2, rb3,
                  send, recv, lsem, psend, precv, vsend, vrecv, isem, osem, wsem,
                  rsend, rrecv, xsend, xrecv, qsend, qrecv, ysend, yrecv, ssend, srecv, free):
     dp = lax.axis_index("dp"); f = lax.axis_index("fsdp")
@@ -110,13 +111,15 @@
     nt = wide // 128
     half = rows // 2
     chips = 4 * Z
-    nz = Z - 1
     ndp = 2 * Z
     hd = wide // HEADS
     full = length // 16 * 16
-    A = pl.ds(0, lanes_a); C = pl.ds(lanes_a, wide - lanes_a)
-    zi = [lax.rem(z + k, Z) for k in range(1, Z)]
-    zs = [(i * 2 + x, f) for i in zi]
+    ta, tb, tc = tiles
+    A = pl.ds(0, ta); B = pl.ds(ta, tb); C = pl.ds(ta + tb, tc)
+    zt = [z + 1 - 2 * (z % 2), lax.rem(z + 2, 4), 3 - z]
+    zd = [(i * 2 + x, f) for i in zt]
+    middle = (z == 1) | (z == 2)
+    ends = (z == 0) | (z == 3)
     xp = (z * 2 + 1 - x, f)
     yp = (dp, (1 - y) * 2 + c)
     pp = (dp, y * 2 + o)
@@ -132,6 +135,10 @@
     for cp in loads: cp.start()
     def remote(src, dst, ssem, rsem, dev):
         return pltpu.make_async_remote_copy(src, dst, ssem, rsem, device_id=dev, device_id_type=MESH)
+    @pl.when(ends)
+    def _():
+        for buf in (ra3, rc2, rb1):
+            for b in range(buf.shape[0]): buf[b, 2] = jnp.zeros(buf.shape[2:], BF)
     floads[0].wait()
     for j in range(nt):
         own[0, :, 128 * j:128 * j + 128] = skip_f[pl.ds(j, rows, stride=nt), :].astype(BF)
@@ -155,61 +162,100 @@
         give[i - 1, 0:half, :] = jnp.where(c == 0, second, first)
         pc[i] = remote(give.at[i - 1], take.at[i - 1], psend.at[i - 1], precv.at[i - 1], pp)
         pc[i].start()
-    def stage1(i):
-        U = unit(i, c)
+    whens = []
+    def cond(cp):
+        whens.append(cp)
+        pl.when(middle)(lambda: cp.start())
+    def zsend(i, base, view):
+        for k in (1, 2, 3):
+            v = view(z)
+            cp = remote(v, v, send.at[i, base + k - 1], recv.at[i, base + k - 1], zd[k - 1])
+            if k == 3: cond(cp)
+            else: cp.start(); waits.append(cp)
+    def zforward(i, base, view):
+        got(i, base + 1, view(zt[1]))
+        v = view(zt[1])
+        cond(remote(v, v, send.at[i, base + 3], recv.at[i, base + 2], zd[0]))
+    def zgot(i, base, view):
+        got(i, base, view(zt[0])); got(i, base + 2, view(zt[2]))
+    lc = {}
+    def ready(i):
         if i in (1, 2, 3, 4):
             pc[i].wait_recv()
             p = keep[i - 1, 0:half, :]
             q = take[i - 1, 0:half, :]
             lo = jnp.where(c == 0, p, q); hi = jnp.where(c == 0, q, p)
             own[i, :, :] = jnp.concatenate([lo, hi], 0).astype(BF)
-        lc[i] = pltpu.make_async_copy(own.at[i], U.at[z, x, y], lsem.at[i]); lc[i].start()
-        rc(i, 2 * nz, own.at[i, :, C], U.at[z, x, y, :, C], yp)
-        for k in range(1, Z):
-            rc(i, k - 1, own.at[i, :, A], U.at[z, x, y, :, A], zs[k - 1])
-    def stage2(i):
+        lc[i] = pltpu.make_async_copy(own.at[i], unit(i, c).at[z, x, y], lsem.at[i]); lc[i].start()
+    SA, SC, SB = 0, 4, 8
+    def gA1(i):
+        U = unit(i, c); lc[i].wait()
+        zsend(i, SA, lambda t: U.at[t, x, y, :, A])
+    def gC1(i):
+        rc(i, 12, own.at[i, :, C], unit(i, c).at[z, x, y, :, C], yp)
+    def gB1(i):
+        rc(i, 13, own.at[i, :, B], unit(i, c).at[z, x, y, :, B], xp)
+    def gAF(i):
+        U = unit(i, c); zforward(i, SA, lambda t: U.at[t, x, y, :, A])
+    def gA2(i):
         U = unit(i, c)
-        lc[i].wait()
-        got(i, 2 * nz, U.at[z, x, 1 - y, :, C])
-        for k in range(1, Z):
-            rc(i, nz + k - 1, U.at[z, x, :, :, C], U.at[z, x, :, :, C], zs[k - 1])
-        for k in range(1, Z):
-            got(i, k - 1, U.at[lax.rem(z - k + Z, Z), x, y, :, A])
+        zgot(i, SA, lambda t: U.at[t, x, y, :, A])
         L = U.at[:, x, y, :, A]
-        rc(i, 2 * nz + 1, L, L, xp)
-        rc(i, 2 * nz + 2, L, L, yp)
-        rc(i, 2 * nz + 5, L, L, pp)
-    def stage3(i):
+        rc(i, 14, L, L, yp); rc(i, 15, L, L, xp); rc(i, 16, L, L, pp)
+    def gA3(i):
+        L = unit(i, c).at[:, 1 - x, y, :, A]
+        got(i, 15, L); rc(i, 17, L, L, yp); rc(i, 18, L, L, pp)
+    def gC2(i):
         U = unit(i, c)
-        for k in range(1, Z):
-            got(i, nz + k - 1, U.at[lax.rem(z - k + Z, Z), x, :, :, C])
+        got(i, 12, U.at[z, x, 1 - y, :, C])
+        zsend(i, SC, lambda t: U.at[t, x, :, :, C])
+    def gCF(i):
+        U = unit(i, c); zforward(i, SC, lambda t: U.at[t, x, :, :, C])
+    def gC3(i):
+        U = unit(i, c)
+        zgot(i, SC, lambda t: U.at[t, x, :, :, C])
         L = U.at[:, x, :, :, C]
-        rc(i, 2 * nz + 4, L, L, xp)
-        rc(i, 2 * nz + 6, L, L, pp)
-        L = U.at[:, 1 - x, y, :, A]
-        got(i, 2 * nz + 1, L)
-        rc(i, 2 * nz + 3, L, L, yp)
-        rc(i, 2 * nz + 7, L, L, pp)
-    def stage4(i):
+        rc(i, 19, L, L, xp); rc(i, 20, L, L, pp)
+    def gB2(i):
+        U = unit(i, c)
+        got(i, 13, U.at[z, 1 - x, y, :, B])
+        L = U.at[z, :, y, :, B]
+        rc(i, 21, L, L, yp)
+    def gB3(i):
+        U = unit(i, c)
+        got(i, 21, U.at[z, :, 1 - y, :, B])
+        zsend(i, SB, lambda t: U.at[t, :, :, :, B])
+    def gBF(i):
+        U = unit(i, c); zforward(i, SB, lambda t: U.at[t, :, :, :, B])
+    def gPA(i):
         U = unit(i, c)
         L = U.at[:, x, 1 - y, :, A]
-        got(i, 2 * nz + 2, L); rc(i, 2 * nz + 8, L, L, pp)
+        got(i, 14, L); rc(i, 22, L, L, pp)
         L = U.at[:, 1 - x, 1 - y, :, A]
-        got(i, 2 * nz + 3, L); rc(i, 2 * nz + 9, L, L, pp)
-        L = U.at[:, 1 - x, :, :, C]
-        got(i, 2 * nz + 4, L); rc(i, 2 * nz + 10, L, L, pp)
+        got(i, 17, L); rc(i, 23, L, L, pp)
+    def gPC(i):
+        L = unit(i, c).at[:, 1 - x, :, :, C]
+        got(i, 19, L); rc(i, 24, L, L, pp)
+    def gPB(i):
+        U = unit(i, c)
+        zgot(i, SB, lambda t: U.at[t, :, :, :, B])
+        L = U.at[:, :, :, :, B]
+        rc(i, 25, L, L, pp)
     def arrived(i):
         U = unit(i, 1 - c)
-        got(i, 2 * nz + 5, U.at[:, x, y, :, A])
-        got(i, 2 * nz + 7, U.at[:, 1 - x, y, :, A])
-        got(i, 2 * nz + 8, U.at[:, x, 1 - y, :, A])
-        got(i, 2 * nz + 9, U.at[:, 1 - x, 1 - y, :, A])
-        got(i, 2 * nz + 6, U.at[:, x, :, :, C])
-        got(i, 2 * nz + 10, U.at[:, 1 - x, :, :, C])
+        got(i, 16, U.at[:, x, y, :, A])
+        got(i, 18, U.at[:, 1 - x, y, :, A])
+        got(i, 22, U.at[:, x, 1 - y, :, A])
+        got(i, 23, U.at[:, 1 - x, 1 - y, :, A])
+        got(i, 20, U.at[:, x, :, :, C])
+        got(i, 24, U.at[:, 1 - x, :, :, C])
+        got(i, 25, U.at[:, :, :, :, B])
     def read(ref, first, stride):
         return jnp.concatenate([ref[pl.ds(first + j, half, stride=stride), :] for j in range(nt)], 1)
 
-    stage1(0)
+    ready(0)
+    gB1(0); gC1(0)
+    gA1(0)
     vcopies = []
     vbuf[dp] = vec_ref[...]
     for k, d in enumerate(dps):
@@ -377,7 +423,11 @@
     started = {j: [] for j in range(7)}
     def sc(j, slot, src, dst, dev):
         cp = remote(src, dst, rsend.at[j, slot], rrecv.at[j, slot], dev)
-        cp.start(); started[j].append(cp)
+        cp.start(); started[j].append((None, cp))
+    def settle(j):
+        for which, cp in started[j]:
+            if which is None: cp.wait_send()
+            else: pl.when(which)(lambda: cp.wait_send())
     def came(j, slot, dst):
         remote(dst, dst, rsend.at[j, slot], rrecv.at[j, slot], pp).wait_recv()
     need = [(0, 1), (2,), (3, 4), (5,), (6, 7), (8, 9), (10, 11)]
@@ -390,71 +440,99 @@
     def reduce1(j):
         for n in need[j]: xcopies[n].wait_recv()
         if j >= nb:
-            for cp in started[j - nb]: cp.wait_send()
+            settle(j - nb)
         b = j % nb
         D = part.at[b]
         l1, r1, l2, r2 = operands(j)
-        step = wide - lanes_a
+        step = SPLIT
         dims = (((0,), (0,)), ((), ()))
         def chunk(n, carry):
-            lanes = pl.ds(pl.multiple_of(n * step, 128), step)
-            r = lax.dot_general(l1[...], r1[:, lanes], dims, preferred_element_type=F32)
-            r = r + lax.dot_general(l2[...], r2[:, lanes], dims, preferred_element_type=F32)
-            D[:, :, :, :, lanes] = r.reshape(Z, 2, 2, rows, step).astype(BF)
+            at = pl.ds(pl.multiple_of(n * step, 128), step)
+            r = lax.dot_general(l1[...], r1[:, at], dims, preferred_element_type=F32)
+            r = r + lax.dot_general(l2[...], r2[:, at], dims, preferred_element_type=F32)
+            D[:, :, :, :, at] = r.reshape(Z, 2, 2, rows, step).astype(BF)
             return carry
         lax.fori_loop(0, wide // step, chunk, 0)
         sc(j, 0, D.at[:, 1 - x, 1 - y, :, A], ra1.at[b, 0], yp)
         sc(j, 2, D.at[:, 1 - x, :, :, C], rc1.at[b], xp)
         sc(j, 1, D.at[:, x, 1 - y, :, A], ra1.at[b, 1], yp)
+        line_send(j, 12, lambda i: D.at[i, :, :, :, B], rb1.at[b], rbf.at[b])
+    def only(j, which, slot, src, dst, dev):
+        cp = remote(src, dst, rsend.at[j, slot], rrecv.at[j, slot], dev)
+        pl.when(which)(lambda: cp.start())
+        return cp
+    def line_send(j, base, view, buf, fbuf):
+        sc(j, base, view(zt[0]), buf.at[0], zd[0])
+        started[j].append((ends, only(j, ends, base + 3, view(zt[2]), fbuf, zd[0])))
+        started[j].append((None, only(j, ends, base + 1, view(zt[1]), buf.at[1], zd[1])))
+        started[j].append((middle, only(j, middle, base + 2, view(zt[2]), buf.at[2], zd[2])))
+    def line_relay(j, base, view, buf, fbuf):
+        cp = remote(view(zt[1]), buf.at[1], rsend.at[j, base + 1], rrecv.at[j, base + 1], zd[1])
+        @pl.when(middle)
+        def _():
+            came(j, base + 3, fbuf)
+            plus(view(zt[1]), fbuf)
+            cp.start()
+    def line_came(j, base, buf):
+        came(j, base, buf.at[0]); came(j, base + 1, buf.at[1])
+        pl.when(middle)(lambda: came(j, base + 2, buf.at[2]))
+    def plus(dst, *srcs):
+        lead = dst.shape[:-2]
+        for n in range(math.prod(lead)):
+            at = ()
+            for d in reversed(lead):
+                at = (n % d,) + at
+                n = n // d
+            v = dst[at + (slice(None), slice(None))].astype(F32)
+            for r in srcs: v = v + r[at + (slice(None), slice(None))].astype(F32)
+            dst[at + (slice(None), slice(None))] = v.astype(BF)
     def reduce2(j):
         b = j % nb
         D = part.at[b]
         came(j, 0, ra1.at[b, 0])
-        for zz in range(Z):
-            va = D.at[zz, 1 - x, y, :, A]
-            va[...] = (va[...].astype(F32) + ra1[b, 0, zz].astype(F32)).astype(BF)
+        plus(D.at[:, 1 - x, y, :, A], ra1.at[b, 0])
         sc(j, 3, D.at[:, 1 - x, y, :, A], ra2.at[b], xp)
         came(j, 2, rc1.at[b])
-        for zz in range(Z):
-            for yy in range(2):
-                va = D.at[zz, x, yy, :, C]
-                va[...] = (va[...].astype(F32) + rc1[b, zz, yy].astype(F32)).astype(BF)
-        for k in range(nz):
-            sc(j, 4 + k, D.at[zi[k], x, :, :, C], rc2.at[b, k], zs[k])
+        plus(D.at[:, x, :, :, C], rc1.at[b])
+        line_send(j, 8, lambda i: D.at[i, x, :, :, C], rc2.at[b], rcf.at[b])
+        line_relay(j, 12, lambda i: D.at[i, :, :, :, B], rb1.at[b], rbf.at[b])
     def reduce3(j):
         b = j % nb
         D = part.at[b]
+        line_came(j, 12, rb1.at[b])
+        plus(D.at[z, :, :, :, B], rb1.at[b, 0], rb1.at[b, 1], rb1.at[b, 2])
+        sc(j, 17, D.at[z, :, 1 - y, :, B], rb2.at[b], yp)
         came(j, 1, ra1.at[b, 1])
         came(j, 3, ra2.at[b])
-        for zz in range(Z):
-            va = D.at[zz, x, y, :, A]
-            va[...] = (va[...].astype(F32) + ra1[b, 1, zz].astype(F32) + ra2[b, zz].astype(F32)).astype(BF)
-        for k in range(nz):
-            sc(j, 4 + nz + k, D.at[zi[k], x, y, :, A], ra3.at[b, k], zs[k])
-        for k in range(nz):
-            came(j, 4 + k, rc2.at[b, k])
-        for yy in range(2):
-            va = D.at[z, x, yy, :, C]
-            s = va[...].astype(F32)
-            for k in range(nz):
-                s = s + rc2[b, k, yy].astype(F32)
-            va[...] = s.astype(BF)
-        sc(j, 4 + 2 * nz, D.at[z, x, 1 - y, :, C], rc3.at[b], yp)
+        plus(D.at[:, x, y, :, A], ra1.at[b, 1], ra2.at[b])
+        line_send(j, 4, lambda i: D.at[i, x, y, :, A], ra3.at[b], raf.at[b])
+        line_relay(j, 8, lambda i: D.at[i, x, :, :, C], rc2.at[b], rcf.at[b])
+    def reduce4(j):
+        b = j % nb
+        D = part.at[b]
+        line_relay(j, 4, lambda i: D.at[i, x, y, :, A], ra3.at[b], raf.at[b])
+        line_came(j, 8, rc2.at[b])
+        plus(D.at[z, x, :, :, C], rc2.at[b, 0], rc2.at[b, 1], rc2.at[b, 2])
+        sc(j, 16, D.at[z, x, 1 - y, :, C], rc3.at[b], yp)
+        came(j, 17, rb2.at[b])
+        plus(D.at[z, :, y, :, B], rb2.at[b])
+        sc(j, 18, D.at[z, 1 - x, y, :, B], rb3.at[b], xp)
     pcopies = {}
     def lay(ref, val, first, stride, n):
         for i in range(val.shape[1] // 128):
             ref[pl.ds(first + i, n, stride=stride), :] = val[:, 128 * i:128 * i + 128]
-    def reduce4(j):
+    def reduce5(j):
         b = j % nb
         D = part.at[b]
-        for k in range(nz):
-            came(j, 4 + nz + k, ra3.at[b, k])
-        came(j, 4 + 2 * nz, rc3.at[b])
-        p = D[z, x, y, :, 0:lanes_a].astype(F32)
-        for k in range(nz):
+        line_came(j, 4, ra3.at[b])
+        came(j, 16, rc3.at[b])
+        came(j, 18, rb3.at[b])
+        p = D[z, x, y, :, A].astype(F32)
+        for k in range(3):
             p = p + ra3[b, k].astype(F32)
-        q = D[z, x, y, :, lanes_a:wide].astype(F32) + rc3[b].astype(F32)
-        v = jnp.concatenate([p, q], 1)
+        q = D[z, x, y, :, B].astype(F32) + rb3[b].astype(F32)
+        r = D[z, x, y, :, C].astype(F32) + rc3[b].astype(F32)
+        v = jnp.concatenate([p, q, r], 1)
         if j in (0, 1):
             lay(fc2_f, v, j * rows * nt, nt, rows)
             if j == 1: keep_out(9, fc2_f, fc2_g)
@@ -471,7 +549,7 @@
         pcopies[j].wait_recv()
         p = keep[j - 2, 0:half, :]; q = take[j - 2, 0:half, :]
         return jnp.where(c == 0, p, q), jnp.where(c == 0, q, p)
-    def reduce5(j):
+    def settle_pair(j):
         if j == 3:
             p, q = both(2), both(3)
             lay(fc1_f, natural_lanes([p[0], q[0], p[1], q[1]], chips), 0, 4 * nt, half)
@@ -618,95 +696,130 @@
             remote(vall.at[src], vall.at[src], ssend.at[k], srecv.at[k], pp).wait_recv()
         vec_o[...] = vall[0] + vall[1] + vall[2] + vall[3]
 
-    stage2(0)
+    ready(1); gB1(1); gB2(0)
+    gC2(0); gAF(0); gA2(0)
+    ready(2); gB1(2)
+    gC1(1); gA1(1); gB2(1)
+    gB3(0)
     prepare_late()
-    stage1(1)
-    stage3(0)
+    gCF(0); gC3(0); gA3(0)
     inputs()
+    gC2(1); gAF(1); gA2(1)
+    ready(3); gB1(3)
+    gC1(2); gA1(2); gB2(2)
+    gB3(1)
     vectors()
-    stage2(1); stage1(2)
-    stage3(1); stage4(0)
+    gCF(1); gC3(1); gA3(1)
+    gBF(0); gPA(0); gPC(0)
+    gC2(2); gAF(2); gA2(2)
+    ready(4); gB1(4)
+    gC1(3); gA1(3); gB2(3)
+    gB3(2)
+    gCF(2); gC3(2); gA3(2)
+    gBF(1); gPA(1); gPC(1)
+    gPB(0)
     first_part()
-    stage2(2); stage1(3)
-    stage3(2); stage4(1)
+    gC2(3); gAF(3); gA2(3)
+    ready(5); gB1(5)
+    gC1(4); gA1(4); gB2(4)
+    gB3(3)
+    gCF(3); gC3(3); gA3(3)
+    gBF(2); gPA(2); gPC(2)
+    gPB(1)
     query_keys()
-    stage2(3); stage1(4)
-    stage3(3); stage4(2)
+    gC2(4); gAF(4); gA2(4)
+    ready(6); gB1(6)
+    gC1(5); gA1(5); gB2(5)
+    gB3(4)
+    gCF(4); gC3(4); gA3(4)
+    gBF(3); gPA(3); gPC(3)
+    gPB(2)
     values()
-    attend(0, 4)
-    stage2(4); stage1(5)
-    attend(4, 11)
-    stage3(4); stage4(3)
+    attend(0, 5)
+    gC2(5); gAF(5); gA2(5)
+    gC1(6); gA1(6); gB2(6)
+    gB3(5)
+    attend(5, 11)
+    gCF(5); gC3(5); gA3(5)
+    gBF(4); gPA(4); gPC(4)
+    gPB(3)
     attend(11, 16)
     second_part()
-    stage2(5); stage1(6)
+    gC2(6); gAF(6); gA2(6)
+    gB3(6)
     widen_load(3)
     widen(0, 0)
-    stage3(5); stage4(4)
+    gCF(6); gC3(6); gA3(6)
+    gBF(5); gPA(5); gPC(5)
+    gPB(4)
     widen(1, 2)
-    stage2(6)
-    widen_load(4)
-    widen(0, 1)
-    stage3(6); stage4(5)
-    widen(1, 3)
     for cp in pc.values(): cp.wait_send()
     swap(0, zz.at[2 * o], xl.at[0])
     swap(1, gm, xr.at[0])
+    swap(3, m, xl.at[2])
+    widen_load(4)
+    reduce1(0)
+    gBF(6); gPA(6); gPC(6); gPB(5)
+    widen(0, 1)
+    widen(1, 3)
     swap(2, zz.at[2 * o + 1], xl.at[1])
-    swap(3, m, xl.at[2])
     narrow_load(5)
-    reduce1(0)
+    reduce1(1)
+    gPB(6)
+    reduce2(0)
     narrow(0, 0)
-    stage4(6)
     narrow(1, 2)
     swap(4, gu.at[2 * o], xr.at[1])
-    reduce1(1); reduce2(0)
     narrow_load(6)
+    reduce1(2); reduce2(1)
     narrow(0, 1)
     narrow(1, 3)
     swap(5, gu.at[2 * o + 1], xr.at[2])
     widen_back_load((0, 1))
-    reduce1(2); reduce2(1); reduce3(0)
+    reduce3(0)
     put_rows(0, acc)
     keep_out(2, tok.at[0], out_o.at[:, 0, :])
+    reduce4(0)
+    reduce1(3)
     widen_back((0, 1))
     widen_back_load((2, 3))
-    reduce1(3)
+    reduce2(2); reduce3(1)
     widen_back((2, 3))
-    reduce2(2); reduce3(1); reduce4(0)
     late_left()
     norm_two()
-    attend_back(0, 4)
-    reduce2(3); reduce3(2); reduce4(1)
-    attend_back(4, 10)
-    reduce3(3); reduce4(2)
-    attend_back(10, 16)
+    reduce5(0); reduce4(1)
+    attend_back(0, 5)
+    reduce2(3); reduce3(2)
+    attend_back(5, 16)
     late_right()
-    reduce1(4); reduce4(3)
+    reduce1(4)
+    reduce5(1); reduce4(2); reduce3(3)
     reduce1(5); reduce2(4)
     project_back()
+    reduce5(2); reduce4(3)
     norm_one()
     vec_send()
+    pltpu.make_async_copy(j_o.at[c], side.at[0], isem.at[7]).wait()
     reduce2(5); reduce3(4)
-    pltpu.make_async_copy(j_o.at[c], side.at[0], isem.at[7]).wait()
     reduce1(6)
     vec_first()
     pltpu.make_async_copy(tok.at[0], out_o.at[:, 0, :], osem.at[2]).wait()
     join_back(0, in_o)
-    reduce3(5); reduce4(4)
+    reduce5(3); reduce4(4)
     join_back(1, sk_o)
-    reduce5(3)
-    reduce2(6)
+    settle_pair(3)
+    reduce2(6); reduce3(5)
     vec_last()
-    reduce4(5); reduce5(4)
+    reduce5(4); reduce4(5); settle_pair(4)
     reduce3(6)
-    reduce5(5)
+    reduce5(5); settle_pair(5)
     reduce4(6)
+    reduce5(6)
     for k in (0, 1): pltpu.make_async_copy(tok.at[k], (in_o, sk_o)[k].at[:, 0, :], osem.at[3 + k]).wait()
     for n, (a, b) in zip((5, 6, 7, 8, 9), ((skip_f, skip_g), (qkv_f, qkv_g), (proj_f, proj_g), (fc1_f, fc1_g), (fc2_f, fc2_g))):
         pltpu.make_async_copy(a, b, osem.at[n]).wait()
-    for j in range(3, 7):
-        for cp in started[j]: cp.wait_send()
+    for j in range(3, 7): settle(j)
+    for cp in whens: pl.when(middle)(lambda: cp.wait_send())
     for cp in waits: cp.wait_send()
     for cp in pcopies.values(): cp.wait_send()
     for cp in vcopies: cp.wait_send()
@@ -717,12 +830,13 @@
     _, length, wide = block_in.shape
     Z = dpn // 2; rows = skip.shape[0] // wide
     padded = -(-length // 16) * 16
-    lanes_a = (wide // 128 * 2 + 1) // 3 * 128
-    lc = wide - lanes_a
+    nt = wide // 128
+    tb = 128 * max(1, nt // 9); tc = 128 * (nt // 3); ta = wide - tb - tc
+    tiles = (ta, tb, tc)
     U = (Z, 2, 2, rows, wide)
     hbm = pl.BlockSpec(memory_space=pl.ANY); vm = pl.BlockSpec(memory_space=pltpu.VMEM)
-    ns = 2 * (Z - 1) + 11
-    nr = 2 * (Z - 1) + 5
+    ns = 26
+    nr = 19
     nv = vectors.shape[0]
     D = pltpu.SemaphoreType.DMA
     V = pltpu.VMEM
@@ -732,9 +846,8 @@
     flat = [(w.shape[0] // 128, 128) for w in (skip, qkv, proj, fc1, fc2)]
     tokens = (length, 1, wide)
     nb = 4
-    nz = Z - 1
     res = pl.pallas_call(
-        functools.partial(block_kernel, Z, wide, rows, lanes_a, length, padded),
+        functools.partial(block_kernel, Z, wide, rows, tiles, length, padded),
         out_shape=(S(tokens, F32),) * 3 + tuple(S(s, F32) for s in flat) + (S((1, nv), F32),
                    S((Z, 2, 2, 2, rows, wide), BF), S((4,) + U, BF), S((4,) + U, BF), S((4,) + U, BF), S((2,) + act, BF), S(act, F32)),
         in_specs=[pl.BlockSpec(memory_space=pltpu.SMEM)] + [hbm] * 5 + [vm] + [hbm] * 3,
@@ -746,8 +859,9 @@
                         V((4,) + act, BF), V((2,) + act, BF), V(act, F32), V((2,) + act, BF), V((3,) + act, BF), V(act, BF), V((4,) + act, BF), V((4,) + act, BF), V(act, BF),
                         V(act, F32), V(act, F32), V((11, 1, wide), F32), V((3, 8, wide), F32), V((2,) + U, BF),
                         V((3,) + act, BF), V((3,) + act, BF), V((nb,) + U, BF),
-                        V((nb, 2, Z, rows, lanes_a), BF), V((nb, Z, rows, lanes_a), BF), V((nb, nz, rows, lanes_a), BF),
-                        V((nb, Z, 2, rows, lc), BF), V((nb, nz, 2, rows, lc), BF), V((nb, rows, lc), BF),
+                        V((nb, 2, Z, rows, ta), BF), V((nb, Z, rows, ta), BF), V((nb, 3, rows, ta), BF), V((nb, rows, ta), BF),
+                        V((nb, Z, 2, rows, tc), BF), V((nb, 3, 2, rows, tc), BF), V((nb, 2, rows, tc), BF), V((nb, rows, tc), BF),
+                        V((nb, 3, 2, 2, rows, tb), BF), V((nb, 2, 2, rows, tb), BF), V((nb, 2, rows, tb), BF), V((nb, rows, tb), BF),
                         D((7, ns)), D((7, ns)), D((7,)), D((4,)), D((4,)), D((dpn - 1,)), D((dpn - 1,)), D((8,)), D((10,)), D((2,)),
                         D((7, nr)), D((7, nr)), D((12,)), D((12,)), D((4,)), D((4,)), D((dpn - 1,)), D((dpn - 1,)), D((3,)), D((3,)), pltpu.SemaphoreType.REGULAR],
         compiler_params=pltpu.CompilerParams(collective_id=0, has_side_effects=True, vmem_limit_bytes=67043328),
@@ -755,12 +869,38 @@
     )(cap, *(w.reshape(-1, 128) for w in (skip, qkv, proj, fc1, fc2)), vectors.reshape(1, nv),
       *(v.reshape(tokens) for v in (block_in, skip_in, out_grad)))
     shape = block_in.shape
-    return tuple(r.reshape(shape) for r in res[:3]) + tuple(r.reshape(-1) for r in res[3:9])
+    res = hand_out(res[:8]) + (res[8],)
+    return tuple(r.reshape(shape) for r in res[:3]) + tuple(r.reshape(-1) for r in res[3:])
+
+
+def hand_out_kernel(*refs):
+    n = (len(refs) - 2) // 3
+    src, dst, buf, (first, second) = refs[:n], refs[n:2 * n], refs[2 * n:3 * n], refs[3 * n:]
+    ins = [pltpu.make_async_copy(src[i], buf[i], first.at[i]) for i in range(n)]
+    outs = [pltpu.make_async_copy(buf[i], dst[i], second.at[i]) for i in range(n)]
+    for cp in ins: cp.start()
+    for a, b in zip(ins, outs):
+        a.wait()
+        b.start()
+    for cp in outs: cp.wait()
+
+
+def hand_out(arrays):
+    hbm = pl.BlockSpec(memory_space=pl.ANY)
+    n = len(arrays)
+    return tuple(pl.pallas_call(
+        hand_out_kernel,
+        out_shape=tuple(jax.ShapeDtypeStruct(v.shape, v.dtype) for v in arrays),
+        in_specs=[hbm] * n, out_specs=(hbm,) * n,
+        scratch_shapes=[pltpu.VMEM(v.shape, v.dtype) for v in arrays] + [pltpu.SemaphoreType.DMA((n,))] * 2,
+        compiler_params=pltpu.CompilerParams(vmem_limit_bytes=67043328),
+        name="hand_out",
+    )(*arrays))
 
 
 def whole_rows(width, dp, fsdp, items, heads, hidden):
     return (
-        fsdp == 4 and dp % 2 == 0 and width % (dp * 16) == 0 and items == 1 and hidden == 4 * width
+        fsdp == 4 and dp == 8 and width % (dp * 16) == 0 and items == 1 and hidden == 4 * width
         and width % SPLIT == 0 and width // heads <= 128
     )
 

time: 390 us -> 365 us (0.936)
  Pallas kernels: 373 us -> 356 us
  local copies, waits for them, and re-layouts: 12.1 us -> 1.3 us
    pallas_call x1 -> x2, Pallas kernels: 373 us -> 356 us  [the longest x1 351 us: block(): pl.pallas_call(functools.partial(block_kernel, Z, wide, rows, tiles, leng...]
    unnamed x22 -> x0, local copies, waits for them, and re-layouts: 10.8 us -> none
where the time goes in v1:
time: 365 us; the launch traced here: 360 us
  Pallas kernels  356 us (98%)
    pallas_call x1, Pallas kernels, block(): pl.pallas_call(functools.partial(block_kernel, Z, wide, rows, tiles, leng...  351 us

profile of v1, /device:TPU:0, one launch (start us, length us, event | category | flops | bytes accessed | tf_op | source)
XLA Modules:
  0.0 360.4 jit_solution(17396932281366019043)
XLA Ops:
  1.3 1.3 reshape.77.vec_ref
  2.6 350.7 %block.1 = (f32[334,1,1152]{2,1,0:T(1,128)}, f32[334,1,1152]{2,1,0:T(1,128)}, f32[334,1,1152]{2,1,0:T(1,128)}, f32[648,128]{1,0:T(8,128)}, f32[972,128]{1,0:T(8,...) custom-call(s32[1]{0:T(128)S(6)} %copy.19.cap_ref, ...), custom_call_target="tpu_custom_call" | custom-call | tf_op jit(solution)/shard_map/block/pallas_call | solution.py:849
  353.3 5.6 %hand_out.1 = (f32[334,1,1152]{2,1,0:T(1,128)}, f32[334,1,1152]{2,1,0:T(1,128)}, f32[334,1,1152]{2,1,0:T(1,128)}, f32[648,128]{1,0:T(8,128)}, f32[972,128]{1,0:T...) custom-call(f32[334,1,1152]{2,1,0:T(1,128)} %get-tuple-element.26.refs_0_, ...), custom_call_target="tpu_custom_call" | custom-call | tf_op jit(solution)/shard_map/hand_out/pallas_call | solution.py:891
  358.9 1.3 reduce

commit v2 on v1

--- a/solution.py
+++ b/solution.py
@@ -75,6 +75,7 @@
 MESH = pl.DeviceIdType.MESH
 BF=jnp.bfloat16; F32=jnp.float32
 SPLIT = 384
+STEP = 112
 
 
 def unit_lanes(value, units, chips):
@@ -99,7 +100,7 @@
 
 def block_kernel(Z, wide, rows, tiles, length, padded,
                  cap_ref, skip_ref, qkv_ref, proj_ref, fc1_ref, fc2_ref, vec_ref, in_ref, sk_ref, og_ref,
-                 out_o, in_o, sk_o, skip_g, qkv_g, proj_g, fc1_g, fc2_g, vec_o, skip_o, qp_o, fc1_o, fc2_o, j_o, h0_o,
+                 out_o, in_o, sk_o, skip_g, qkv_g, proj_g, fc1_g, fc2_g, vec_o, skip_o, qp_o, fc1_o, fc2_o, j_o, h0_o, acc_o,
                  skip_f, qkv_f, proj_f, fc1_f, fc2_f, own, keep, give, take, vbuf, vecs, b1s, vpart, vgot, vall, tok,
                  dtg, side, hid, am, t, m, zz, gu, gm, acc, tmp, sums, gacc, wbuf,
                  xl, xr, part, ra1, ra2, ra3, raf, rc1, rc2, rcf, rc3, rb1, rbf, rb2, rb3,
@@ -304,7 +305,7 @@
             cen = v - jnp.mean(v, -1, keepdims=True)
             s = jnp.mean(cen * cen, -1, keepdims=True)
             dst[r, :] = (cen * lax.rsqrt(s + epsilon) * gain + shift).astype(BF)
-        row_loop(padded, 16, one)
+        row_loop(padded, STEP, one)
     def take_rows(k, dst, at):
         if padded > full: dst[at + (slice(padded - 16, padded), slice(None))] = jnp.zeros((16, wide), dst.dtype)
         def one(r): dst[at + (r, slice(None))] = tok[k, r, :].astype(dst.dtype)
@@ -319,7 +320,7 @@
             u = unit_lanes(jnp.concatenate([dtg[0, r, :], dtg[1, r, :]], 1), 2, chips)
             side[0, r, :] = u[0]
             side[1, r, :] = u[1]
-        row_loop(padded, 16, two)
+        row_loop(padded, STEP, two)
         keep_out(0, side, j_o)
     def vectors():
         for k in range(len(dps)):
@@ -348,9 +349,11 @@
     def query_keys():
         arrived(1)
         for u in range(2): weight(u, qp_o.at[u])
-        for u in range(2):
+        def each(u, carry):
             weight_wait(u)
             project(u, u)
+            return carry
+        lax.fori_loop(0, 2, each, 0)
     def values():
         arrived(2)
         weight(0, qp_o.at[2]); weight(1, qp_o.at[3])
@@ -384,10 +387,16 @@
             hid[:, l] = h
             acc[:, l] = h + vecs[0:1, pl.ds(6 * wide + l.start, SPLIT)]
         lanes_loop(one)
+        keep_out(10, acc, acc_o)
         norm(hid, vector(2), vector(3), m)
     def widen_load(i):
         arrived(i)
         for k in range(2): weight(k, fc1_o.at[2 * k + i - 3])
+    def pair_loop(fn, first):
+        def one(k, carry):
+            fn(k, 2 * k + first)
+            return carry
+        lax.fori_loop(0, 2, one, 0)
     def widen(k, u):
         weight_wait(k)
         def one(l):
@@ -399,7 +408,7 @@
             pdf = jnp.exp(-0.5 * v * v) * 0.3989422804014327
             zz[u, r, :] = (v * cdf).astype(BF)
             gu[u, r, :] = (cdf + v * pdf).astype(BF)
-        row_loop(padded, 16, two)
+        row_loop(padded, STEP, two)
     def narrow_load(i):
         arrived(i)
         for k in range(2): weight(k, fc2_o.at[2 * k + i - 5])
@@ -407,13 +416,27 @@
         weight_wait(k)
         tmp[...] = jnp.zeros_like(tmp)
         def one(l):
-            w = cols(k, l)
-            acc[:, l] += jnp.dot(zz[u], w, preferred_element_type=F32)
-            tmp[...] += lax.dot_general(gm[:, l], w, (((1,), (1,)), ((), ())), preferred_element_type=F32)
+            tmp[...] += lax.dot_general(gm[:, l], cols(k, l), (((1,), (1,)), ((), ())), preferred_element_type=F32)
         lanes_loop(one)
         def two(r):
             gu[u, r, :] = (tmp[r, :] * gu[u, r, :].astype(F32)).astype(BF)
-        row_loop(padded, 16, two)
+        row_loop(padded, STEP, two)
+    def finish():
+        pltpu.make_async_copy(acc_o, acc, isem.at[8]).wait()
+        for u in range(2): weight(u, fc2_o.at[u])
+        def each(u, carry):
+            k = u % 2
+            weight_wait(k)
+            def one(l):
+                acc[:, l] += jnp.dot(zz[u], cols(k, l), preferred_element_type=F32)
+            lanes_loop(one)
+            pl.when(u < 2)(lambda: weight(k, fc2_o.at[u + 2]))
+            return carry
+        lax.fori_loop(0, 4, each, 0)
+    def finish_out():
+        pltpu.make_async_copy(tok.at[0], in_o.at[:, 0, :], osem.at[3]).wait()
+        put_rows(0, acc)
+        keep_out(2, tok.at[0], out_o.at[:, 0, :])
 
     xcopies = {}
     def swap(n, src, dst):
@@ -568,13 +591,13 @@
 
     def zero(n): gacc[n] = jnp.zeros((8, wide), F32)
     def add_rows(n, v):
-        gacc[n] += v[0:8] + v[8:16]
+        gacc[n] += jnp.sum(v.reshape(v.shape[0] // 8, 8, wide), 0)
     def close(n):
         return jnp.sum(gacc[n], 0, keepdims=True)
     def column_sums(src):
         zero(0)
         def one(r): add_rows(0, src[r, :].astype(F32))
-        row_loop(padded, 16, one)
+        row_loop(padded, STEP, one)
         return close(0)
     def norm_back(dy, src, gain, fn):
         zero(0); zero(1); zero(2)
@@ -589,22 +612,26 @@
             add_rows(0, d * xh)
             add_rows(1, d)
             fn(r, g)
-        row_loop(padded, 16, one)
+        row_loop(padded, STEP, one)
     def turned(lhs, n, fresh):
         if fresh: tmp[...] = jnp.zeros_like(tmp)
         def one(l):
             tmp[...] += lax.dot_general(lhs[:, l], cols(n, l), (((1,), (1,)), ((), ())), preferred_element_type=F32)
         lanes_loop(one)
-    def widen_back(us):
-        for i, u in enumerate(us):
-            weight_wait(i)
-            turned(gu.at[u], i, u == 0)
+    def widen_back():
+        tmp[...] = jnp.zeros_like(tmp)
+        def each(u, carry):
+            k = u % 2
+            weight_wait(k)
+            turned(gu.at[u], k, False)
+            pl.when(u < 2)(lambda: weight(k, fc1_o.at[u + 2]))
             sums[7 + u] = column_sums(gu.at[u])
-    def widen_back_load(us):
-        for i, u in enumerate(us): weight(i, fc1_o.at[u])
+            return carry
+        lax.fori_loop(0, 4, each, 0)
     def norm_two():
         weight(0, qp_o.at[3])
         pltpu.make_async_copy(og_ref.at[:, 0, :], tok.at[1], isem.at[6]).wait()
+        pltpu.make_async_copy(acc, acc_o, osem.at[10]).wait()
         take_rows(1, acc, ())
         def fn(r, g):
             s = acc[r, :] + g
@@ -619,7 +646,7 @@
         weight_wait(0)
         turned(dtg.at[3], 0, True)
         def two(r): side[0, r, :] = tmp[r, :].astype(BF)
-        row_loop(padded, 16, two)
+        row_loop(padded, STEP, two)
     def attend_back(first, last):
         cap = cap_ref[0]
         key = lax.broadcasted_iota(jnp.int32, (padded, 1), 0)
@@ -655,10 +682,14 @@
         pltpu.make_async_copy(j_o.at[c], side.at[0], isem.at[7]).start()
         weight(0, qp_o.at[0]); weight(1, qp_o.at[1])
     def project_back():
-        for i in range(3):
-            weight_wait(i % 2)
-            turned(dtg.at[i], i % 2, i == 0)
-            if i == 0: weight(0, qp_o.at[2])
+        tmp[...] = jnp.zeros_like(tmp)
+        def each(i, carry):
+            k = i % 2
+            weight_wait(k)
+            turned(dtg.at[i], k, False)
+            pl.when(i == 0)(lambda: weight(0, qp_o.at[2]))
+            return carry
+        lax.fori_loop(0, 3, each, 0)
     def norm_one():
         pltpu.make_async_copy(h0_o, hid, isem.at[5]).wait()
         both_skip()
@@ -669,6 +700,7 @@
         norm_back(tmp, hid, vector(0), fn)
         sums[0] = close(0); sums[1] = close(1); sums[4] = close(2)
         swap(11, side.at[1], xr.at[2])
+        pltpu.make_async_copy(acc_o, acc, isem.at[8]).start()
     def join_back(i, dst):
         weight_wait(i)
         turned(side.at[1], i, True)
@@ -760,31 +792,24 @@
     widen_load(4)
     reduce1(0)
     gBF(6); gPA(6); gPC(6); gPB(5)
-    widen(0, 1)
-    widen(1, 3)
+    pair_loop(widen, 1)
     swap(2, zz.at[2 * o + 1], xl.at[1])
     narrow_load(5)
     reduce1(1)
     gPB(6)
     reduce2(0)
-    narrow(0, 0)
-    narrow(1, 2)
+    pair_loop(narrow, 0)
     swap(4, gu.at[2 * o], xr.at[1])
     narrow_load(6)
     reduce1(2); reduce2(1)
-    narrow(0, 1)
-    narrow(1, 3)
+    pair_loop(narrow, 1)
     swap(5, gu.at[2 * o + 1], xr.at[2])
-    widen_back_load((0, 1))
+    weight(0, fc1_o.at[0]); weight(1, fc1_o.at[1])
     reduce3(0)
-    put_rows(0, acc)
-    keep_out(2, tok.at[0], out_o.at[:, 0, :])
     reduce4(0)
     reduce1(3)
-    widen_back((0, 1))
-    widen_back_load((2, 3))
     reduce2(2); reduce3(1)
-    widen_back((2, 3))
+    widen_back()
     late_left()
     norm_two()
     reduce5(0); reduce4(1)
@@ -803,19 +828,21 @@
     reduce2(5); reduce3(4)
     reduce1(6)
     vec_first()
-    pltpu.make_async_copy(tok.at[0], out_o.at[:, 0, :], osem.at[2]).wait()
     join_back(0, in_o)
     reduce5(3); reduce4(4)
     join_back(1, sk_o)
     settle_pair(3)
-    reduce2(6); reduce3(5)
+    reduce3(5); reduce2(6)
     vec_last()
     reduce5(4); reduce4(5); settle_pair(4)
+    finish()
+    finish_out()
     reduce3(6)
     reduce5(5); settle_pair(5)
     reduce4(6)
     reduce5(6)
-    for k in (0, 1): pltpu.make_async_copy(tok.at[k], (in_o, sk_o)[k].at[:, 0, :], osem.at[3 + k]).wait()
+    pltpu.make_async_copy(tok.at[1], sk_o.at[:, 0, :], osem.at[4]).wait()
+    pltpu.make_async_copy(tok.at[0], out_o.at[:, 0, :], osem.at[2]).wait()
     for n, (a, b) in zip((5, 6, 7, 8, 9), ((skip_f, skip_g), (qkv_f, qkv_g), (proj_f, proj_g), (fc1_f, fc1_g), (fc2_f, fc2_g))):
         pltpu.make_async_copy(a, b, osem.at[n]).wait()
     for j in range(3, 7): settle(j)
@@ -849,9 +876,9 @@
     res = pl.pallas_call(
         functools.partial(block_kernel, Z, wide, rows, tiles, length, padded),
         out_shape=(S(tokens, F32),) * 3 + tuple(S(s, F32) for s in flat) + (S((1, nv), F32),
-                   S((Z, 2, 2, 2, rows, wide), BF), S((4,) + U, BF), S((4,) + U, BF), S((4,) + U, BF), S((2,) + act, BF), S(act, F32)),
+                   S((Z, 2, 2, 2, rows, wide), BF), S((4,) + U, BF), S((4,) + U, BF), S((4,) + U, BF), S((2,) + act, BF), S(act, F32), S(act, F32)),
         in_specs=[pl.BlockSpec(memory_space=pltpu.SMEM)] + [hbm] * 5 + [vm] + [hbm] * 3,
-        out_specs=(hbm,) * 8 + (vm,) + (hbm,) * 6,
+        out_specs=(hbm,) * 8 + (vm,) + (hbm,) * 7,
         scratch_shapes=[V(s, F32) for s in flat] + [
                         V((7, rows, wide), BF), V((4, hp, wide), F32), V((4, hp, wide), F32), V((4, hp, wide), F32),
                         V((dpn, 1, nv), F32), V((1, nv * dpn), F32), V((4, 1, wide), F32), V((dpn, 1, nv), F32), V((dpn - 1, 1, nv), F32), V((4, 1, nv), F32),
@@ -862,7 +889,7 @@
                         V((nb, 2, Z, rows, ta), BF), V((nb, Z, rows, ta), BF), V((nb, 3, rows, ta), BF), V((nb, rows, ta), BF),
                         V((nb, Z, 2, rows, tc), BF), V((nb, 3, 2, rows, tc), BF), V((nb, 2, rows, tc), BF), V((nb, rows, tc), BF),
                         V((nb, 3, 2, 2, rows, tb), BF), V((nb, 2, 2, rows, tb), BF), V((nb, 2, rows, tb), BF), V((nb, rows, tb), BF),
-                        D((7, ns)), D((7, ns)), D((7,)), D((4,)), D((4,)), D((dpn - 1,)), D((dpn - 1,)), D((8,)), D((10,)), D((2,)),
+                        D((7, ns)), D((7, ns)), D((7,)), D((4,)), D((4,)), D((dpn - 1,)), D((dpn - 1,)), D((9,)), D((11,)), D((2,)),
                         D((7, nr)), D((7, nr)), D((12,)), D((12,)), D((4,)), D((4,)), D((dpn - 1,)), D((dpn - 1,)), D((3,)), D((3,)), pltpu.SemaphoreType.REGULAR],
         compiler_params=pltpu.CompilerParams(collective_id=0, has_side_effects=True, vmem_limit_bytes=67043328),
         name="block",
@@ -898,16 +925,16 @@
     )(*arrays))
 
 
-def whole_rows(width, dp, fsdp, items, heads, hidden):
+def whole_rows(width, dp, fsdp, items, heads, hidden, length):
     return (
         fsdp == 4 and dp == 8 and width % (dp * 16) == 0 and items == 1 and hidden == 4 * width
-        and width % SPLIT == 0 and width // heads <= 128
+        and width % SPLIT == 0 and -(-length // 16) * 16 % STEP == 0 and width // heads <= 128
     )
 
 
 def body(block_in, skip_in, out_grad, caption_len, skip_w, qkv_w, proj_w, fc1_w, fc2_w, vectors):
     items, length, width = block_in.shape
-    if whole_rows(width, lax.axis_size("dp"), lax.axis_size("fsdp"), items, HEADS, FF):
+    if whole_rows(width, lax.axis_size("dp"), lax.axis_size("fsdp"), items, HEADS, FF, length):
         return block(
             caption_len, skip_w, qkv_w, proj_w, fc1_w, fc2_w, vectors, block_in, skip_in, out_grad,
             lax.axis_size("dp"),

time: 365 us -> 350 us (0.959); the launches traced: 360 us -> 349 us
  Pallas kernels: 356 us -> 346 us
    pallas_call x1, Pallas kernels: 351 us -> 340 us  [block(): pl.pallas_call(functools.partial(block_kernel, Z, wide, rows, tiles, leng...]
where the time goes in v2:
time: 350 us; the launch traced here: 349 us
  Pallas kernels  346 us (99%)
    pallas_call x1, Pallas kernels, block(): pl.pallas_call(functools.partial(block_kernel, Z, wide, rows, tiles, leng...  340 us

profile of v2, /device:TPU:0, one launch (start us, length us, event | category | flops | bytes accessed | tf_op | source)
XLA Modules:
  0.0 349.5 jit_solution(2099229822400270317)
XLA Ops:
  1.3 1.3 reshape.77.vec_ref
  2.6 340.0 %block.1 = (f32[334,1,1152]{2,1,0:T(1,128)}, f32[334,1,1152]{2,1,0:T(1,128)}, f32[334,1,1152]{2,1,0:T(1,128)}, f32[648,128]{1,0:T(8,128)}, f32[972,128]{1,0:T(8,...) custom-call(s32[1]{0:T(128)S(6)} %copy.19.cap_ref, ...), custom_call_target="tpu_custom_call" | custom-call | tf_op jit(solution)/shard_map/block/pallas_call | solution.py:876
  342.6 5.6 %hand_out.1 = (f32[334,1,1152]{2,1,0:T(1,128)}, f32[334,1,1152]{2,1,0:T(1,128)}, f32[334,1,1152]{2,1,0:T(1,128)}, f32[648,128]{1,0:T(8,128)}, f32[972,128]{1,0:T...) custom-call(f32[334,1,1152]{2,1,0:T(1,128)} %get-tuple-element.26.refs_0_, ...), custom_call_target="tpu_custom_call" | custom-call | tf_op jit(solution)/shard_map/hand_out/pallas_call | solution.py:918
  348.2 1.3 reduce

commit v3 on v2

--- a/solution.py
+++ b/solution.py
@@ -258,9 +258,9 @@
     gB1(0); gC1(0)
     gA1(0)
     vcopies = []
-    vbuf[dp] = vec_ref[...]
+    vbuf[dp] = vec_ref[...].reshape(1, vec_ref.shape[0])
     for k, d in enumerate(dps):
-        cp = remote(vec_ref, vbuf.at[dp], vsend.at[k], vrecv.at[k], d)
+        cp = remote(vbuf.at[dp], vbuf.at[dp], vsend.at[k], vrecv.at[k], d)
         cp.start(); vcopies.append(cp)
     floads[1].wait(); floads[2].wait()
     exchange(1, read(qkv_f, 0, 3 * nt), read(qkv_f, nt, 3 * nt))
@@ -324,7 +324,7 @@
         keep_out(0, side, j_o)
     def vectors():
         for k in range(len(dps)):
-            remote(vec_ref, vbuf.at[lax.rem(dp - (k + 1) + ndp, ndp)], vsend.at[k], vrecv.at[k], pp).wait_recv()
+            remote(vbuf.at[dp], vbuf.at[lax.rem(dp - (k + 1) + ndp, ndp)], vsend.at[k], vrecv.at[k], pp).wait_recv()
         vecs[...] = jnp.concatenate([vbuf[k] for k in range(ndp)], 1)
         b = unit_lanes(vecs[0:1, 7 * wide:11 * wide], 4, chips)
         for u in range(4): b1s[u] = b[u]
@@ -460,7 +460,7 @@
         if j == 4: return am.at[c], dtg.at[2 + c], xl.at[0], xr.at[0]
         if j == 5: return am.at[0], dtg.at[c], xl.at[1], xr.at[1]
         return side.at[0], side.at[1], xl.at[2], xr.at[2]
-    def reduce1(j):
+    def partial(j):
         for n in need[j]: xcopies[n].wait_recv()
         if j >= nb:
             settle(j - nb)
@@ -476,6 +476,12 @@
             D[:, :, :, :, at] = r.reshape(Z, 2, 2, rows, step).astype(BF)
             return carry
         lax.fori_loop(0, wide // step, chunk, 0)
+    def reduce1(j):
+        partial(j)
+        ship(j)
+    def ship(j):
+        b = j % nb
+        D = part.at[b]
         sc(j, 0, D.at[:, 1 - x, 1 - y, :, A], ra1.at[b, 0], yp)
         sc(j, 2, D.at[:, 1 - x, :, :, C], rc1.at[b], xp)
         sc(j, 1, D.at[:, x, 1 - y, :, A], ra1.at[b, 1], yp)
@@ -726,7 +732,7 @@
         for k in range(3):
             src = lax.rem(f - (k + 1) + 4, 4)
             remote(vall.at[src], vall.at[src], ssend.at[k], srecv.at[k], pp).wait_recv()
-        vec_o[...] = vall[0] + vall[1] + vall[2] + vall[3]
+        vec_o[...] = (vall[0] + vall[1] + vall[2] + vall[3]).reshape(vec_o.shape[0])
 
     ready(1); gB1(1); gB2(0)
     gC2(0); gAF(0); gA2(0)
@@ -801,11 +807,11 @@
     pair_loop(narrow, 0)
     swap(4, gu.at[2 * o], xr.at[1])
     narrow_load(6)
+    reduce3(0)
     reduce1(2); reduce2(1)
     pair_loop(narrow, 1)
     swap(5, gu.at[2 * o + 1], xr.at[2])
     weight(0, fc1_o.at[0]); weight(1, fc1_o.at[1])
-    reduce3(0)
     reduce4(0)
     reduce1(3)
     reduce2(2); reduce3(1)
@@ -875,7 +881,7 @@
     nb = 4
     res = pl.pallas_call(
         functools.partial(block_kernel, Z, wide, rows, tiles, length, padded),
-        out_shape=(S(tokens, F32),) * 3 + tuple(S(s, F32) for s in flat) + (S((1, nv), F32),
+        out_shape=(S(tokens, F32),) * 3 + tuple(S(s, F32) for s in flat) + (S((nv,), F32),
                    S((Z, 2, 2, 2, rows, wide), BF), S((4,) + U, BF), S((4,) + U, BF), S((4,) + U, BF), S((2,) + act, BF), S(act, F32), S(act, F32)),
         in_specs=[pl.BlockSpec(memory_space=pltpu.SMEM)] + [hbm] * 5 + [vm] + [hbm] * 3,
         out_specs=(hbm,) * 8 + (vm,) + (hbm,) * 7,
@@ -893,10 +899,10 @@
                         D((7, nr)), D((7, nr)), D((12,)), D((12,)), D((4,)), D((4,)), D((dpn - 1,)), D((dpn - 1,)), D((3,)), D((3,)), pltpu.SemaphoreType.REGULAR],
         compiler_params=pltpu.CompilerParams(collective_id=0, has_side_effects=True, vmem_limit_bytes=67043328),
         name="block",
-    )(cap, *(w.reshape(-1, 128) for w in (skip, qkv, proj, fc1, fc2)), vectors.reshape(1, nv),
+    )(cap, *(w.reshape(-1, 128) for w in (skip, qkv, proj, fc1, fc2)), vectors,
       *(v.reshape(tokens) for v in (block_in, skip_in, out_grad)))
     shape = block_in.shape
-    res = hand_out(res[:8]) + (res[8],)
+    res = hand_out(res[:9])
     return tuple(r.reshape(shape) for r in res[:3]) + tuple(r.reshape(-1) for r in res[3:])
 
 

time: 350 us -> 348 us (level)
  no operation moved by 1% of the time
where the time goes in v3:
time: 348 us; the launch traced here: 347 us
  Pallas kernels  346 us (99%)
    pallas_call x1, Pallas kernels, block(): pl.pallas_call(functools.partial(block_kernel, Z, wide, rows, tiles, leng...  340 us

profile of v3, /device:TPU:0, one launch (start us, length us, event | category | flops | bytes accessed | tf_op | source)
XLA Modules:
  0.0 347.3 jit_solution(16791291533783808108)
XLA Ops:
  1.3 340.2 %block.1 = (f32[334,1,1152]{2,1,0:T(1,128)}, f32[334,1,1152]{2,1,0:T(1,128)}, f32[334,1,1152]{2,1,0:T(1,128)}, f32[648,128]{1,0:T(8,128)}, f32[972,128]{1,0:T(8,...) custom-call(s32[1]{0:T(128)S(6)} %copy.19.cap_ref, ...), custom_call_target="tpu_custom_call" | custom-call | tf_op jit(solution)/shard_map/block/pallas_call | solution.py:882
  341.5 5.6 %hand_out.1 = (f32[334,1,1152]{2,1,0:T(1,128)}, f32[334,1,1152]{2,1,0:T(1,128)}, f32[334,1,1152]{2,1,0:T(1,128)}, f32[648,128]{1,0:T(8,128)}, f32[972,128]{1,0:T...) custom-call(f32[334,1,1152]{2,1,0:T(1,128)} %get-tuple-element.27.refs_0_, ...), custom_call_target="tpu_custom_call" | custom-call | tf_op jit(solution)/shard_map/hand_out/pallas_call | solution.py:924

commit v4 on v3

--- a/solution.py
+++ b/solution.py
@@ -739,8 +739,8 @@
     ready(2); gB1(2)
     gC1(1); gA1(1); gB2(1)
     gB3(0)
+    gCF(0); gC3(0); gA3(0)
     prepare_late()
-    gCF(0); gC3(0); gA3(0)
     inputs()
     gC2(1); gAF(1); gA2(1)
     ready(3); gB1(3)

time: 348 us -> 345 us (level)
  no operation moved by 1% of the time
where the time goes in v4:
time: 345 us
  Pallas kernels  343 us (99%)
    pallas_call x1, Pallas kernels, block(): pl.pallas_call(functools.partial(block_kernel, Z, wide, rows, tiles, leng...  338 us

profile of v4, /device:TPU:0, one launch (start us, length us, event | category | flops | bytes accessed | tf_op | source)
XLA Modules:
  0.0 344.9 jit_solution(11131950907114773040)
XLA Ops:
  1.3 337.8 %block.1 = (f32[334,1,1152]{2,1,0:T(1,128)}, f32[334,1,1152]{2,1,0:T(1,128)}, f32[334,1,1152]{2,1,0:T(1,128)}, f32[648,128]{1,0:T(8,128)}, f32[972,128]{1,0:T(8,...) custom-call(s32[1]{0:T(128)S(6)} %copy.19.cap_ref, ...), custom_call_target="tpu_custom_call" | custom-call | tf_op jit(solution)/shard_map/block/pallas_call | solution.py:882
  339.1 5.6 %hand_out.1 = (f32[334,1,1152]{2,1,0:T(1,128)}, f32[334,1,1152]{2,1,0:T(1,128)}, f32[334,1,1152]{2,1,0:T(1,128)}, f32[648,128]{1,0:T(8,128)}, f32[972,128]{1,0:T...) custom-call(f32[334,1,1152]{2,1,0:T(1,128)} %get-tuple-element.27.refs_0_, ...), custom_call_target="tpu_custom_call" | custom-call | tf_op jit(solution)/shard_map/hand_out/pallas_call | solution.py:924
